TPU v7x, 128 devices: a whole 4x4x4 slice. The times are simulated.
128 devices in a mesh: lev: 8 (over z, y_lo), mem: 16 (over x, y_hi, core).
Axes of the slice: x: 4, y: 4 (y_hi: 2, y_lo: 2; y = y_hi * 2 + y_lo), z: 4, core: 2. Of those that a mesh axis runs over, the one named last changes fastest.
Arguments:
- perturbations: bfloat16 [64, 2, 128, 256, 256], P('mem', None, 'lev'), may hold values from -6 to 6
- gradient: bfloat16 [2, 128, 256, 256], P(None, 'lev', 'mem'), may hold values from -6 to 6
- member_scale: int32 [64], P('mem'), may hold values from 0 to 3
- kernel_y: bfloat16 [4, 256, 256], replicated, may hold values from 0 to 1, as said below
- kernel_x: bfloat16 [4, 256, 256], replicated, may hold values from 0 to 1, as said below
- vertical_weights: float32 [4, 5], replicated, may hold values from 0.2 to 1
- layer_index: int32 [128], replicated, may hold values from 0 to 15, never falling along the last dimension, each value on 1 to 16 neighbouring positions
Outputs:
- increment: float32 [2, 128, 256, 256], P(None, 'lev', 'mem')
Inputs may be any that keep to these rules, and one draw needn't show every extreme that they name: `layer_index`: layer numbers never fall from one level to the next; every layer has at least one level and at most 16. `kernel_y`: each scale's matrix has nonnegative entries and rows that sum to one. `kernel_x`: each scale's matrix has nonnegative entries and rows that sum to one.
All inputs are finite; a program needn't handle non-finite values.
Results may differ from a plain program's by a relative error of at most 0.0039.
Values may be sent and summed in bfloat16 or wider, within the bound.
No kernel may reach another device: no remote copies, remote signals or barrier semaphores. Data moves between devices by JAX's collectives and lax.ppermute only.
A program may use at most 128 MiB of HBM per device.

v0:
```python
import jax
import jax.numpy as jnp
from jax import lax
from jax.sharding import PartitionSpec as P

SCALES = 4


def with_halo(block, sides, width):
    for axis, dim in sides:
        count = lax.axis_size(axis)
        forward = [(i, i + 1) for i in range(count - 1)]
        backward = [(target, source) for source, target in forward]
        low = lax.ppermute(
            lax.slice_in_dim(block, block.shape[dim] - width, None, axis=dim), axis, forward
        )
        high = lax.ppermute(lax.slice_in_dim(block, 0, width, axis=dim), axis, backward)
        block = jnp.concatenate([low, block, high], axis=dim)
    return block


def select_tables(member_scale, kernel_y, kernel_x, vertical_weights):
    chosen = member_scale[:, None] == jnp.arange(SCALES, dtype=jnp.int32)[None, :]
    pick_half = chosen.astype(jnp.bfloat16)
    rows_table = jnp.einsum(
        "ms,sij->mij", pick_half, kernel_y, preferred_element_type=jnp.float32
    ).astype(jnp.bfloat16)
    cols_table = jnp.einsum(
        "ms,sij->mij", pick_half, kernel_x, preferred_element_type=jnp.float32
    ).astype(jnp.bfloat16)
    weights = jnp.dot(chosen.astype(jnp.float32), vertical_weights, precision=lax.Precision.HIGHEST)
    return (rows_table, cols_table, weights)


def horizontal(members, gradient, rows_table, cols_table):
    product = (
        members.astype(jnp.float32)
        * lax.all_gather(gradient, "mem", axis=2, tiled=True)[None].astype(jnp.float32)
    ).astype(jnp.bfloat16)
    summed = jnp.einsum("mij,mvljx->mvlix", rows_table, product, preferred_element_type=jnp.float32)
    smoothed = summed.astype(jnp.bfloat16)
    return jnp.einsum(
        "mvlib,mab->mvlia", smoothed, cols_table, preferred_element_type=jnp.float32
    ).astype(jnp.bfloat16)


def vertical(extended, weights, local_ids, levels):
    shape = (extended.shape[0], extended.shape[1], levels, extended.shape[3], extended.shape[4])
    total = jnp.zeros(shape, jnp.float32)
    centre = local_ids[2 : 2 + levels]
    for offset in range(-2, 3):
        same = (local_ids[2 + offset : 2 + offset + levels] == centre).astype(jnp.float32)
        factor = weights[:, offset + 2][:, None, None, None, None] * same[None, None, :, None, None]
        total = total + factor * extended[:, :, 2 + offset : 2 + offset + levels].astype(
            jnp.float32
        )
    return total


def per_device(
    perturbations, gradient, member_scale, kernel_y, kernel_x, vertical_weights, layer_index
):
    count = perturbations.shape[0]
    levels = perturbations.shape[2]
    rows_table, cols_table, weights = select_tables(
        member_scale, kernel_y, kernel_x, vertical_weights
    )
    padded_ids = jnp.pad(layer_index, 2, constant_values=-1)
    local_ids = lax.dynamic_slice_in_dim(padded_ids, lax.axis_index("lev") * levels, levels + 4)
    local_field = horizontal(perturbations, gradient, rows_table, cols_table)
    extended = with_halo(local_field, (("lev", 2),), 2)
    mixed = vertical(extended, weights, local_ids, levels)
    members_all = count * lax.axis_size("mem")
    terms = jnp.sum(perturbations.astype(jnp.float32) * mixed, axis=0) / (members_all - 1)
    return lax.psum_scatter(terms, "mem", scatter_dimension=2, tiled=True)


def solution(mesh):
    placed = (
        P("mem", None, "lev", None, None),
        P(None, "lev", "mem", None),
        P("mem"),
        P(),
        P(),
        P(),
        P(),
    )
    return jax.shard_map(
        per_device,
        mesh=mesh,
        in_specs=placed,
        out_specs=P(None, "lev", "mem", None),
        check_vma=False,
    )
```

profile of v0, /device:TPU:0, one launch (start us, length us, event | category | flops | bytes accessed | tf_op | source)
XLA Modules:
  0.0 367.0 jit_solution(18009959018631775468)
XLA Ops:
  6.5 0.7 all-gather.2.cloned.1.call-update
  7.3 0.0 reduce-scatter.2.cloned.1.call-start
  7.3 0.3 copy-done
  7.6 1.2 fusion.27
  8.8 1.6 fusion.25
  10.4 60.2 %all-gather.2.cloned.1.call-done = bf16[2,16,256,256]{3,2,1,0:T(8,128)(2,1)} async-done(((bf16[2,16,16,256]{3,2,1,0:T(8,128)(2,1)}), bf16[2,16,256,256]{3,2,1,0:T(8,128)(2,1)}) %all-gather.2.cloned.1.call-update) | async-done | bytes 4194320 | tf_op jit(solution)/shard_map/all_gather | solution.py:38
  70.6 6.5 %convert_element_type.60 = f32[2,16,256,256]{3,2,1,0:T(8,128)} convert(bf16[2,16,256,256]{3,2,1,0:T(8,128)(2,1)} %all-gather.2.cloned.1.call-done) | non-fusion elementwise | flops 2097152 | bytes 12582912 | tf_op jit(solution)/shard_map/convert_element_type | solution.py:38
  77.1 19.2 %fusion.15 = bf16[4,2,16,256,256]{4,3,2,1,0:T(8,128)(2,1)} fusion(bf16[4,2,16,256,256]{4,3,2,1,0:T(8,128)(2,1)} %param.7, f32[2,16,256,256]{3,2,1,0:T(8,128)} %convert_element_type.60, bf16[4,256,256]{2,0,1:T(4,128)(2,1)S(1)} %fusion.27, bf16[4,256,256]{2,0,1:T(4,128)(2,1)S(1)} %fusion.25), kind=kOutput, calls=%fused_computation.17 | convolution fusion | flops 8631877632 | bytes 42991616 | tf_op jit(solution)/shard_map/mvlib,mab->mvlia/dot_general | solution.py:42
  96.3 4.6 %fusion.36 = (bf16[4,2,2,256,256]{4,3,2,1,0:T(8,128)(2,1)}, bf16[4,2,2,256,256]{4,3,2,1,0:T(8,128)(2,1)}) fusion(bf16[4,2,16,256,256]{4,3,2,1,0:T(8,128)(2,1)} %fusion.15), kind=kLoop, calls=%fused_computation.47 | loop fusion | bytes 8388608 | tf_op jit(solution)/shard_map/slice | solution.py:15
  100.9 2.6 collective-permute-start
  103.5 1.3 collective-permute-start.1
  104.8 0.1 pad_dynamic-slice_fusion
  104.9 0.0 copy-done.2
  104.9 0.2 fusion.30
  105.1 0.2 slice_reduce_fusion.4
  105.3 0.1 compare_convert_fusion.3
  105.4 0.1 broadcast_multiply_fusion.3
  105.5 0.1 broadcast_multiply_fusion.1
  105.5 43.4 %collective-permute-done = bf16[4,2,2,256,256]{4,3,2,1,0:T(8,128)(2,1)S(1)} collective-permute-done((bf16[4,2,2,256,256]{4,3,2,1,0:T(8,128)(2,1)}, bf16[4,2,2,256,256]{4,3,2,1,0:T(8,128)(2,1)S(1)}, u32[]{:S(2)}, u32[]{:S(2)}) %collective-permute-start) | collective-permute-done | bytes 2097184 | tf_op jit(solution)/shard_map/ppermute | solution.py:14
  149.0 47.8 %collective-permute-done.1 = bf16[4,2,2,256,256]{4,3,2,1,0:T(8,128)(2,1)} collective-permute-done((bf16[4,2,2,256,256]{4,3,2,1,0:T(8,128)(2,1)}, bf16[4,2,2,256,256]{4,3,2,1,0:T(8,128)(2,1)}, u32[]{:S(2)}, u32[]{:S(2)}) %collective-permute-start.1) | collective-permute-done | bytes 2097184 | tf_op jit(solution)/shard_map/ppermute | solution.py:17
  196.8 54.7 %fusion.1 = f32[2,16,256,256]{3,2,1,0:T(8,128)} fusion(bf16[4,2,16,256,256]{4,3,2,1,0:T(8,128)(2,1)} %param.7, bf16[4,2,16,256,256]{4,3,2,1,0:T(8,128)(2,1)} %fusion.15, bf16[4,2,2,256,256]{4,3,2,1,0:T(8,128)(2,1)} %collective-permute-done.1, bf16[4,2,2,256,256]{4,3,2,1,0:T(8,128)(2,1)S(1)} %collective-permute-done, f32[4,16]{1,0:T(4,128)S(1)} %get-tuple-element.16, ...), kind=kLoop, calls=%fused_computation.3 | loop fusion | flops 174063616 | bytes 46138384 | tf_op jit(solution)/shard_map/reduce_sum | solution.py:74
  251.5 7.8 %broadcast_multiply_fusion = f32[2,16,256,256]{3,2,1,0:T(8,128)} fusion(f32[2,16,256,256]{3,2,1,0:T(8,128)} %fusion.1), kind=kLoop, calls=%fused_computation.18 | loop fusion | flops 2097152 | bytes 16777216 | tf_op jit(solution)/shard_map/div | solution.py:74
  259.3 0.0 reduce-scatter.2.cloned.1.call-update
  259.3 100.8 %reduce-scatter.2.cloned.1.call-done = f32[2,16,16,256]{3,2,1,0:T(8,128)} async-done(((f32[2,16,256,256]{3,2,1,0:T(8,128)}), f32[2,16,16,256]{3,2,1,0:T(8,128)}) %reduce-scatter.2.cloned.1.call-update) | async-done | bytes 524304 | tf_op jit(solution)/shard_map/reduce_scatter | solution.py:75
  (9 shorter events, 0.0 us)
Async XLA Ops:
  6.5 1.0 copy-start
  6.5 64.0 %all-gather.2.cloned.1.call-start = ((), (), s32[]{:S(2)}) async-start(), calls=%async_computation.1 | async-start | bytes 4456448 | tf_op jit(solution)/shard_map/all_gather | solution.py:38
  7.3 352.9 %reduce-scatter.2.cloned.1.call-start = ((), (), s32[]{:S(2)}) async-start(), calls=%async_computation.2 | async-start | bytes 8912896 | tf_op jit(solution)/shard_map/reduce_scatter | solution.py:75
  77.0 27.8 %copy-start.3 = (s32[128]{0:T(128)S(1)}, s32[128]{0:T(128)}, u32[]{:S(2)}) copy-start(s32[128]{0:T(128)} %param.13) | copy-start | bytes 1540
  77.0 27.8 %copy-start.2 = (f32[4,5]{1,0:T(4,128)S(1)}, f32[4,5]{1,0:T(4,128)}, u32[]{:S(2)}) copy-start(f32[4,5]{1,0:T(4,128)} %param.12) | copy-start | bytes 244
  77.1 27.8 %copy-start.4 = (s32[4]{0:T(128)S(1)}, s32[4]{0:T(128)}, u32[]{:S(2)}) copy-start(s32[4]{0:T(128)} %param.9) | copy-start | bytes 52
  100.9 48.1 %collective-permute-start = (bf16[4,2,2,256,256]{4,3,2,1,0:T(8,128)(2,1)}, bf16[4,2,2,256,256]{4,3,2,1,0:T(8,128)(2,1)S(1)}, u32[]{:S(2)}, u32[]{:S(2)}) collective-permute-start(bf16[4,2,2,256,256]{4,3,2,1,0:T(8,128)(2,1)} %get-tuple-element.10), channel_id=1, source_target_pairs={{0,16},{16,32},{32,48},{48,64},{64,80},{80,96},{96,112},{1,17},{17... | collective-permute-start | bytes 6291464 | tf_op jit(solution)/shard_map/ppermute | solution.py:14
  103.5 93.3 %collective-permute-start.1 = (bf16[4,2,2,256,256]{4,3,2,1,0:T(8,128)(2,1)}, bf16[4,2,2,256,256]{4,3,2,1,0:T(8,128)(2,1)}, u32[]{:S(2)}, u32[]{:S(2)}) collective-permute-start(bf16[4,2,2,256,256]{4,3,2,1,0:T(8,128)(2,1)} %get-tuple-element.11), channel_id=1, source_target_pairs={{16,0},{32,16},{48,32},{64,48},{80,64},{96,80},{112,96},{17,1},{33... | collective-permute-start | bytes 6291464 | tf_op jit(solution)/shard_map/ppermute | solution.py:17
  196.8 163.4 %copy-start.1 = (bf16[4,256,256]{2,1,0:T(8,128)(2,1)S(1)}, bf16[4,256,256]{2,1,0:T(8,128)(2,1)}, u32[]{:S(2)}) copy-start(bf16[4,256,256]{2,1,0:T(8,128)(2,1)} %param.10) | copy-start | bytes 1572868
Sparse Core Ops, SparseCore 0:
  9.6 60.9 all-gather.1
  259.4 100.6 reduce-scatter.1
where the time goes:
time: 367 us
  waiting for transfers between devices  253 us (69%)
  other arithmetic  69.2 us (19%)
  matrix products  22.2 us (6%)
  between operations  13.5 us (4%)
  local copies, waits for them, and re-layouts  5.18 us (1%)
  starting transfers between devices  3.94 us (1%)
    reduce_scatter x1, waiting for transfers between devices, per_device(): return lax.psum_scatter(terms, 'mem', scatter_dimension=2, tiled=True)  101 us
    all_gather x1, waiting for transfers between devices, horizontal(): lax.all_gather(gradient, 'mem', axis=2, tiled=True)[None]  60.2 us
    reduce_sum x1, other arithmetic, per_device(): jnp.sum(perturbations.astype(jnp.float32) * mixed, axis=0)  54.7 us
    ppermute x1, waiting for transfers between devices, with_halo(): lax.ppermute(lax.slice_in_dim(block, 0, width, axis=dim), axis, backward)  47.8 us
    ppermute x1, waiting for transfers between devices, with_halo(): lax.ppermute(lax.slice_in_dim(block, block.shape[dim] - width, None, axis...  43.4 us
    dot_general x1, matrix products, horizontal(): jnp.einsum('mvlib,mab->mvlia', smoothed, cols_table, preferred_element_ty...  19.2 us
    div x1, other arithmetic, per_device(): jnp.sum(perturbations.astype(jnp.float32) * mixed, axis=0)  7.77 us
  transfers between devices with their start and end apart: 4, of which 4 were waited for; matrix products, arithmetic and copies ran while one was open for 1% of the time, Pallas kernels for 0%

commit v1 on v0

v1 whole, which is shorter than its diff:
```python
import functools

import jax
import jax.numpy as jnp
from jax import lax
from jax.experimental import pallas as pl
from jax.experimental.pallas import tpu as pltpu
from jax.sharding import PartitionSpec as P


NXC, NH, NC = 4, 2, 2
BF = jnp.bfloat16
F32 = jnp.float32


def pairs_of(dx, dh, dc):
    out = []
    for x in range(NXC):
        for h in range(NH):
            for c in range(NC):
                dest = ((x + dx) % NXC) * 4 + ((h + dh) % NH) * 2 + (c + dc) % NC
                out.append((x * 4 + h * 2 + c, dest))
    return out


def move(value, dx=0, dh=0, dc=0):
    return lax.ppermute(value, "mem", pairs_of(dx, dh, dc))


def shift(value, pairs):
    return lax.ppermute(value, "lev", pairs)


def rows_at(mem, j, hr, cr):
    x = mem // 4
    h = (mem // 2) % 2
    c = mem % 2
    block = ((x + j) % 4) * 4 + ((h + hr) % 2) * 2 + (c + cr) % 2
    return pl.multiple_of(block * 16, 16)


def field(p, g, ky, kxt):
    product = p * g
    rows = jnp.dot(ky, product, preferred_element_type=F32).astype(BF)
    return jnp.dot(rows, kxt, preferred_element_type=F32).astype(BF)


def own_kernel(
    ms_ref, li_ref, ids_ref, w_ref, p_ref, q_ref, ky_ref, kxt_ref, *rest, levels, inv
):
    pieces = rest[:8]
    send_ref, keep_ref, hedge_ref, gs, acc, *rings = rest[8:]
    t = pl.program_id(0)
    mem = ids_ref[0]
    base = ids_ref[1] * levels

    @pl.when(t == 0)
    def _():
        for ring in rings:
            for slot in (3, 4):
                ring[slot] = jnp.zeros(ring.shape[1:], F32)

    lo = t - 2
    level = jnp.minimum(t, levels - 1)
    newest = lax.rem(t, 5)
    slots = [lax.rem(t + 1 + d, 5) for d in range(5)]

    def coef(k, d):
        other = lo + d
        a = jnp.clip(base + lo, 0, 127)
        b = jnp.clip(base + other, 0, 127)
        ok = (other >= 0) & (other < levels) & (li_ref[a] == li_ref[b])
        return jnp.where(ok, w_ref[ms_ref[k], d + 2], 0.0) * inv

    for cr in range(2):
        for hr in range(2):
            for j in range(4):
                block = pieces[cr * 4 + j][hr * levels + level]
                gs[pl.ds(rows_at(mem, j, hr, cr), 16), :] = block
    g = gs[...]

    for k in range(4):
        s = ms_ref[k]
        rings[k][newest] = field(p_ref[k, 0, 0], g, ky_ref[s], kxt_ref[s]).astype(F32)
        cs = [coef(k, d) for d in range(-2, 3)]
        for cr in range(2):
            for hr in range(2):
                for j in range(4):
                    place = cr * 8 + hr * 4 + j
                    r0 = rows_at(mem, j, hr, cr)
                    mix = None
                    for d in range(5):
                        term = cs[d] * rings[k][slots[d], pl.ds(r0, 16), :]
                        mix = term if mix is None else mix + term
                    mix = mix * q_ref[k, 0, 0, pl.ds(r0, 16), :].astype(F32)
                    if k:
                        mix = mix + acc[place]
                    if k < 3:
                        acc[place] = mix
                    elif cr:
                        send_ref[0, j, hr] = mix.astype(BF)
                    else:
                        keep_ref[0, j, hr] = mix

    @pl.when((t == 1) | (t == levels - 2))
    def _():
        for k in range(4):
            hedge_ref[0, k] = rings[k][newest].astype(BF)


def own_part(v, ms, li, ids, w, p, ky, kxt, pieces, inv):
    levels = p.shape[2]
    smem = pl.BlockSpec(memory_space=pltpu.SMEM)
    whole = pl.BlockSpec((4, 256, 256), lambda t, *_: (0, 0, 0))
    pblock = (4, 1, 1, 256, 256)
    part = pl.BlockSpec((1, 4, 2, 16, 256), lambda t, *_: (jnp.maximum(t - 2, 0), 0, 0, 0, 0))
    return pl.pallas_call(
        functools.partial(own_kernel, levels=levels, inv=inv),
        grid_spec=pltpu.PrefetchScalarGridSpec(
            num_scalar_prefetch=3,
            grid=(levels + 2,),
            in_specs=[
                smem,
                pl.BlockSpec(pblock, lambda t, *_: (0, v, jnp.minimum(t, levels - 1), 0, 0)),
                pl.BlockSpec(pblock, lambda t, *_: (0, v, jnp.maximum(t - 2, 0), 0, 0)),
                whole,
                whole,
            ]
            + [pl.BlockSpec((2 * levels, 16, 256), lambda t, *_: (0, 0, 0))] * 8,
            out_specs=[
                part,
                part,
                pl.BlockSpec(
                    (1, 4, 256, 256), lambda t, *_: (jnp.where(t < levels - 2, 0, 1), 0, 0, 0)
                ),
            ],
            scratch_shapes=[
                pltpu.VMEM((256, 256), BF),
                pltpu.VMEM((16, 16, 256), F32),
            ]
            + [pltpu.VMEM((5, 256, 256), F32)] * 4,
        ),
        out_shape=[
            jax.ShapeDtypeStruct((levels, 4, 2, 16, 256), BF),
            jax.ShapeDtypeStruct((levels, 4, 2, 16, 256), F32),
            jax.ShapeDtypeStruct((2, 4, 256, 256), BF),
        ],
    )(ms, li, ids, w, p, p, ky, kxt, *pieces)


def edge_kernel(
    ms_ref, li_ref, ids_ref, w_ref, above_ref, below_ref, first_ref, last_ref, ky_ref, kxt_ref,
    hedge_ref, *rest, v, levels, inv
):
    pieces = rest[:8]
    send_ref, keep_ref, gs, hs = rest[8:]
    mem = ids_ref[0]
    base = ids_ref[1] * levels
    for side in range(2):
        top = side == 0
        halo_ref = above_ref if top else below_ref
        p_ref = first_ref if top else last_ref
        for cr in range(2):
            for j in range(4):
                piece = pieces[cr * 4 + j]
                gs[side, pl.ds(rows_at(mem, j, 0, cr), 16), :] = piece[4 + side * 2 + v]
                gs[side, pl.ds(rows_at(mem, j, 1, cr), 16), :] = piece[side * 2 + v]
        g = gs[side]
        for k in range(4):
            s = ms_ref[k]
            hs[side, k] = field(halo_ref[k, 0], g, ky_ref[s], kxt_ref[s]).astype(F32)
    for side in range(2):
        top = side == 0
        halo_ref = above_ref if top else below_ref
        p_ref = first_ref if top else last_ref
        far = base - 1 if top else base + levels
        near = base if top else base + levels - 1
        after = base + 1 if top else base + levels - 2
        inside = (far >= 0) & (far < 128)
        far_id = li_ref[jnp.clip(far, 0, 127)]
        ok1 = inside & (far_id == li_ref[near])
        ok2 = inside & (far_id == li_ref[after])

        def pick(k, place, ok):
            return jnp.where(ok, w_ref[ms_ref[k], place], 0.0) * inv

        c_near = [pick(k, 1 if top else 3, ok1) for k in range(4)]
        c_next = [pick(k, 0 if top else 4, ok2) for k in range(4)]
        c_back = [pick(k, 4 if top else 0, ok2) for k in range(4)]
        i_near = 0 if top else 1
        for cr in range(2):
            for j in range(4):
                for hr in range(2):
                    rows = pl.ds(rows_at(mem, j, hr, cr), 16)
                    a, b, e = None, None, None
                    for k in range(4):
                        h = hs[side, k, rows, :]
                        a_k = c_near[k] * (h * p_ref[k, 0, i_near, rows, :].astype(F32))
                        b_k = c_next[k] * (h * p_ref[k, 0, 1 - i_near, rows, :].astype(F32))
                        e_k = c_back[k] * (
                            hedge_ref[side, k, rows, :].astype(F32)
                            * halo_ref[k, 0, rows, :].astype(F32)
                        )
                        a = a_k if a is None else a + a_k
                        b = b_k if b is None else b + b_k
                        e = e_k if e is None else e + e_k
                    places = (0, 1) if top else (3, 2)
                    for n, value in zip((*places, 4 + side), (a, b, e)):
                        if cr:
                            send_ref[n, j, hr] = value.astype(BF)
                        else:
                            keep_ref[n, j, hr] = value


def edge_part(v, ms, li, ids, w, above, below, p, ky, kxt, hedges, lasts, inv):
    levels = p.shape[2]
    smem = pl.BlockSpec(memory_space=pltpu.SMEM)
    whole = pl.BlockSpec((4, 256, 256), lambda t, *_: (0, 0, 0))
    halo = pl.BlockSpec((4, 1, 256, 256), lambda t, *_: (0, v, 0, 0))
    part = pl.BlockSpec((6, 4, 2, 16, 256), lambda t, *_: (0, 0, 0, 0, 0))
    return pl.pallas_call(
        functools.partial(edge_kernel, v=v, levels=levels, inv=inv),
        grid_spec=pltpu.PrefetchScalarGridSpec(
            num_scalar_prefetch=3,
            grid=(1,),
            in_specs=[
                smem,
                halo,
                halo,
                pl.BlockSpec((4, 1, 2, 256, 256), lambda t, *_: (0, v, 0, 0, 0)),
                pl.BlockSpec((4, 1, 2, 256, 256), lambda t, *_: (0, v, levels // 2 - 1, 0, 0)),
                whole,
                whole,
                pl.BlockSpec((2, 4, 256, 256), lambda t, *_: (0, 0, 0, 0)),
            ]
            + [pl.BlockSpec((8, 16, 256), lambda t, *_: (2 * levels // 8, 0, 0))] * 8,
            out_specs=[part, part],
            scratch_shapes=[
                pltpu.VMEM((2, 256, 256), BF),
                pltpu.VMEM((2, 4, 256, 256), F32),
            ],
        ),
        out_shape=[
            jax.ShapeDtypeStruct((6, 4, 2, 16, 256), BF),
            jax.ShapeDtypeStruct((6, 4, 2, 16, 256), F32),
        ],
    )(ms, li, ids, w, above, below, p, p, ky, kxt, hedges, *lasts)


def gather_x(payload):
    got = {j: move(payload, dx=-j) for j in (1, 3, 2)}
    return [payload, got[1], got[2], got[3]]


def gather_c(pieces):
    return pieces + [move(piece, dc=1) for piece in pieces]


def scatter_rows(total):
    got = [move(total[:, j].astype(BF), dx=j) for j in (1, 3, 2)]
    mine = total[:, 0]
    for piece in got:
        mine = mine + piece.astype(F32)
    return mine[:, 0] + move(mine[:, 1].astype(BF), dh=1).astype(F32)


def per_device(
    perturbations, gradient, member_scale, kernel_y, kernel_x, vertical_weights, layer_index
):
    levels = perturbations.shape[2]
    inv = 1.0 / (perturbations.shape[0] * lax.axis_size("mem") - 1)
    count = lax.axis_size("lev")
    up = [(i, i + 1) for i in range(count - 1)]
    down = [(i + 1, i) for i in range(count - 1)]
    ids = jnp.stack([lax.axis_index("mem"), lax.axis_index("lev")]).astype(jnp.int32)
    kxt = jnp.swapaxes(kernel_x, 1, 2)

    other = [move(gradient[v], dh=1) for v in range(2)]
    g_halo = jnp.concatenate(
        [shift(gradient[:, levels - 1], up), shift(gradient[:, 0], down)],
        axis=0,
    )
    x0 = gather_x(jnp.concatenate([gradient[0], other[0]]))
    other_halo = move(g_halo, dh=1)
    x1 = gather_x(jnp.concatenate([gradient[1], other[1], other_halo, g_halo]))
    pieces = [gather_c(x0), gather_c(x1)]
    above = shift(perturbations[:, :, levels - 1], up)
    below = shift(perturbations[:, :, 0], down)

    outs = []
    for v in range(2):
        send, keep, hedges = own_part(
            v, member_scale, layer_index, ids, vertical_weights, perturbations,
            kernel_y, kxt, pieces[v], inv,
        )
        own = keep + move(send, dc=1).astype(F32)
        send, keep = edge_part(
            v, member_scale, layer_index, ids, vertical_weights, above, below,
            perturbations, kernel_y, kxt, hedges, pieces[1], inv,
        )
        edge = keep + move(send, dc=1).astype(F32)
        total = jnp.concatenate(
            [
                own[:2] + edge[:2],
                own[2 : levels - 2],
                own[levels - 2 :] + edge[2:4],
                edge[4:],
            ]
        )
        mine = scatter_rows(total)
        from_above = shift(mine[levels + 1], up)
        from_below = shift(mine[levels], down)
        outs.append(
            jnp.concatenate(
                [
                    (mine[0] + from_above)[None],
                    mine[1 : levels - 1],
                    (mine[levels - 1] + from_below)[None],
                ]
            )
        )
    return jnp.stack(outs)


def solution(mesh):
    placed = (
        P("mem", None, "lev", None, None),
        P(None, "lev", "mem", None),
        P("mem"),
        P(),
        P(),
        P(),
        P(),
    )
    return jax.shard_map(
        per_device,
        mesh=mesh,
        in_specs=placed,
        out_specs=P(None, "lev", "mem", None),
        check_vma=False,
    )
```

time: 367 us -> 185 us (0.50)
  waiting for transfers between devices: 253 us -> 44 us
  other arithmetic: 69.2 us -> 6.68 us
  Pallas kernels: 0 us -> 59.6 us
  starting transfers between devices: 3.94 us -> 56.7 us
  matrix products: 22.2 us -> 0 us
  between operations: 13.5 us -> 0.54 us
  local copies, waits for them, and re-layouts: 5.18 us -> 15 us
    reduce_scatter x1 -> x0, waiting for transfers between devices: 101 us -> none  [per_device(): return lax.psum_scatter(terms, 'mem', scatter_dimension=2, tiled=True)]
    all_gather x1 -> x0, waiting for transfers between devices: 60.2 us -> none  [horizontal(): lax.all_gather(gradient, 'mem', axis=2, tiled=True)[None]]
    pallas_call x0 -> x4, Pallas kernels: none -> 59.6 us  [the longest x2 47.5 us: own_part(): pl.pallas_call(functools.partial(own_kernel, levels=levels, inv=inv), gri...]
    reduce_sum x1 -> x0, other arithmetic: 54.7 us -> none  [per_device(): jnp.sum(perturbations.astype(jnp.float32) * mixed, axis=0)]
    ppermute x2 -> x37, starting transfers between devices: 3.9 us -> 56.7 us  [the longest x29 32.9 us: move(): return lax.ppermute(value, 'mem', pairs_of(dx, dh, dc))]
    ppermute x2 -> x37, waiting for transfers between devices: 91.3 us -> 44 us  [the longest x29 36.9 us: move(): return lax.ppermute(value, 'mem', pairs_of(dx, dh, dc))]
    dot_general x4 -> x0, matrix products: 22.2 us -> none  [the longest x1 19.2 us: horizontal(): jnp.einsum('mvlib,mab->mvlia', smoothed, cols_table, preferred_element_ty...]
    div x1 -> x0, other arithmetic: 7.77 us -> none  [per_device(): jnp.sum(perturbations.astype(jnp.float32) * mixed, axis=0)]
  transfers between devices with their start and end apart: 4 -> 37, of which waited for: 4 -> 16; matrix products, arithmetic and copies ran while one was open for 1% -> 9% of each run, Pallas kernels for 0% -> 33%
where the time goes in v1:
time: 185 us; the launch traced here: 183 us
  Pallas kernels  59.6 us (32%)
  starting transfers between devices  56.7 us (31%)
  waiting for transfers between devices  44 us (24%)
  local copies, waits for them, and re-layouts  15 us (8%)
  other arithmetic  6.68 us (4%)
    pallas_call x2, Pallas kernels, own_part(): pl.pallas_call(functools.partial(own_kernel, levels=levels, inv=inv), gri...  47.5 us
    ppermute x29, waiting for transfers between devices, move(): return lax.ppermute(value, 'mem', pairs_of(dx, dh, dc))  36.9 us
    ppermute x29, starting transfers between devices, move(): return lax.ppermute(value, 'mem', pairs_of(dx, dh, dc))  32.9 us
    ppermute x8, starting transfers between devices, shift(): return lax.ppermute(value, 'lev', pairs)  23.8 us
    pallas_call x2, Pallas kernels, edge_part(): pl.pallas_call(functools.partial(edge_kernel, v=v, levels=levels, inv=inv...  12.1 us
    ppermute x8, waiting for transfers between devices, shift(): return lax.ppermute(value, 'lev', pairs)  7.15 us
    unnamed x43, local copies, waits for them, and re-layouts  6.27 us
  transfers between devices with their start and end apart: 37, of which 16 were waited for; matrix products, arithmetic and copies ran while one was open for 9% of the time, Pallas kernels for 33%

profile of v1, /device:TPU:0, one launch (start us, length us, event | category | flops | bytes accessed | tf_op | source)
XLA Modules:
  0.0 182.6 jit_solution(12348996709492145881)
XLA Ops:
  0.7 3.6 %collective-permute-start.12 = (bf16[2,16,256]{2,1,0:T(8,128)(2,1)S(1)}, bf16[2,16,256]{2,1,0:T(8,128)(2,1)S(1)}, u32[]{:S(2)}, u32[]{:S(2)}) collective-permute-start(bf16[2,16,256]{2,1,0:T(8,128)(2,1)S(1)} %get-tuple-element.49), channel_id=1, source_target_pairs={{0,16},{16,32},{32,48},{48,64},{64,80},{80,96},{96,112},{1,17},{17... | collective-permute-start | bytes 49160 | tf_op jit(solution)/shard_map/ppermute | solution.py:31
  6.6 3.0 %collective-permute-start.11 = (bf16[16,16,256]{2,1,0:T(8,128)(2,1)S(1)}, bf16[16,16,256]{2,1,0:T(8,128)(2,1)S(1)}, u32[]{:S(2)}, u32[]{:S(2)}) collective-permute-start(bf16[16,16,256]{2,1,0:T(8,128)(2,1)S(1)} %get-tuple-element.48), channel_id=1, source_target_pairs={{0,2},{1,3},{2,0},{3,1},{4,6},{5,7},{6,4},{7,5},{8,10},{9,11},{10,... | collective-permute-start | bytes 393224 | tf_op jit(solution)/shard_map/ppermute | solution.py:27
  11.2 3.0 %collective-permute-start.14 = (bf16[4,16,256]{2,1,0:T(8,128)(2,1)S(1)}, bf16[4,16,256]{2,1,0:T(8,128)(2,1)S(1)}, u32[]{:S(2)}, u32[]{:S(2)}) collective-permute-start(bf16[4,16,256]{2,1,0:T(8,128)(2,1)S(1)} %pad_maximum_fusion.4), channel_id=1, source_target_pairs={{0,2},{1,3},{2,0},{3,1},{4,6},{5,7},{6,4},{7,5},{8,10},{9,11},{10,... | collective-permute-start | bytes 98312 | tf_op jit(solution)/shard_map/ppermute | solution.py:27
  14.2 2.2 %collective-permute-done = bf16[16,16,256]{2,1,0:T(8,128)(2,1)S(1)} collective-permute-done((bf16[16,16,256]{2,1,0:T(8,128)(2,1)S(1)}, bf16[16,16,256]{2,1,0:T(8,128)(2,1)S(1)}, u32[]{:S(2)}, u32[]{:S(2)}) %collective-permute-start) | collective-permute-done | bytes 131104 | tf_op jit(solution)/shard_map/ppermute | solution.py:27
  18.0 2.7 %collective-permute-start.2 = (bf16[32,16,256]{2,1,0:T(8,128)(2,1)S(1)}, bf16[32,16,256]{2,1,0:T(8,128)(2,1)S(1)}, u32[]{:S(2)}, u32[]{:S(2)}) collective-permute-start(bf16[32,16,256]{2,1,0:T(8,128)(2,1)S(1)} %pad_maximum_fusion.3.rest_0_), channel_id=1, source_target_pairs={{0,8},{1,9},{2,10},{3,11},{4,12},{5,13},{6,14},{7,15},{8,0},{9,1},... | collective-permute-start | bytes 786440 | tf_op jit(solution)/shard_map/ppermute | solution.py:27
  22.4 3.1 %slice_bitcast_fusion = (bf16[4,2,256,256]{3,2,1,0:T(8,128)(2,1)}, bf16[4,2,256,256]{3,2,1,0:T(8,128)(2,1)}) fusion(bf16[4,2,16,256,256]{4,3,2,1,0:T(8,128)(2,1)} %last_ref.3), kind=kLoop, calls=%fused_computation.4 | loop fusion | bytes 4194304 | tf_op jit(solution)/shard_map/squeeze | solution.py:288
  26.8 5.2 %collective-permute-start.9 = (bf16[4,2,256,256]{3,2,1,0:T(8,128)(2,1)}, bf16[4,2,256,256]{3,2,1,0:T(8,128)(2,1)S(1)}, u32[]{:S(2)}, u32[]{:S(2)}) collective-permute-start(bf16[4,2,256,256]{3,2,1,0:T(8,128)(2,1)} %get-tuple-element.26), channel_id=1, source_target_pairs={{0,16},{16,32},{32,48},{48,64},{64,80},{80,96},{96,112},{1,17},{17... | collective-permute-start | bytes 3145736 | tf_op jit(solution)/shard_map/ppermute | solution.py:31
  33.0 2.6 %collective-permute-start.16 = (bf16[40,16,256]{2,1,0:T(8,128)(2,1)S(1)}, bf16[40,16,256]{2,1,0:T(8,128)(2,1)S(1)}, u32[]{:S(2)}, u32[]{:S(2)}) collective-permute-start(bf16[40,16,256]{2,1,0:T(8,128)(2,1)S(1)} %constant_dynamic-update-slice_fusion.rest_0_), channel_id=1, source_target_pairs={{0,8},{1,9},{2,10},{3,11},{4,12},{5,13},{6,14},{7,15},{8,0},{9,1},... | collective-permute-start | bytes 983048 | tf_op jit(solution)/shard_map/ppermute | solution.py:27
  37.1 13.3 %collective-permute-done.17.rest_3_ = bf16[40,16,256]{2,1,0:T(8,128)(2,1)S(1)} collective-permute-done((bf16[40,16,256]{2,1,0:T(8,128)(2,1)S(1)}, bf16[40,16,256]{2,1,0:T(8,128)(2,1)S(1)}, u32[]{:S(2)}, u32[]{:S(2)}) %collective-permute-start.17) | collective-permute-done | bytes 327712 | tf_op jit(solution)/shard_map/ppermute | solution.py:27
  53.4 2.0 %copy.8 = bf16[4,256,256]{1,2,0:T(8,128)(2,1)} copy(bf16[4,256,256]{2,1,0:T(8,128)(2,1)} %param.11) | data formatting | bytes 1048576 | tf_op args[4]
  56.1 23.7 %shard_map.73 = (bf16[16,4,2,16,256]{4,3,2,1,0:T(8,128)(2,1)}, f32[16,4,2,16,256]{4,3,2,1,0:T(8,128)}, bf16[2,4,256,256]{3,2,1,0:T(8,128)(2,1)}) custom-call(s32[4]{0:T(128)} %ms_ref.7, s32[128]{0:T(128)} %li_ref.7, s32[2]{0:T(128)} %pad_add_fusion.ids_ref, f32[4,5]{1,0:T(4,128)} %w_ref.7, bf16[4,2,16,256,256]{4,3,2,1,0:T(8,128)(2,1)} %last_ref.3, ...), custom_call_target="tpu_custom_call" | custom-call | tf_op jit(solution)/shard_map/pallas_call | solution.py:117
  79.8 2.3 %copy.9 = bf16[16,4,2,16,256]{4,3,0,2,1:T(8,128)(2,1)} copy(bf16[16,4,2,16,256]{4,3,2,1,0:T(8,128)(2,1)} %get-tuple-element.16) | data formatting | bytes 2097152 | tf_op jit(solution)/shard_map/pallas_call | solution.py:117
  83.7 5.9 %shard_map.74 = (bf16[6,4,2,16,256]{4,3,2,1,0:T(8,128)(2,1)}, f32[6,4,2,16,256]{4,3,2,1,0:T(8,128)}) custom-call(s32[4]{0:T(128)} %ms_ref.7, s32[128]{0:T(128)} %li_ref.7, s32[2]{0:T(128)} %pad_add_fusion.ids_ref, f32[4,5]{1,0:T(4,128)} %w_ref.7, bf16[4,2,256,256]{3,2,1,0:T(8,128)(2,1)} %copy-done.1, bf16[4,2,256,256]{3,2,1,0:T(8,128)(2,1)} %copy-done, ...), custom_call_target="tpu_custom_call" | custom-call | tf_op jit(solution)/shard_map/pallas_call | solution.py:221
  91.3 23.8 %shard_map.75 = (bf16[16,4,2,16,256]{4,3,2,1,0:T(8,128)(2,1)}, f32[16,4,2,16,256]{4,3,2,1,0:T(8,128)}, bf16[2,4,256,256]{3,2,1,0:T(8,128)(2,1)}) custom-call(s32[4]{0:T(128)} %ms_ref.7, s32[128]{0:T(128)} %li_ref.7, s32[2]{0:T(128)} %pad_add_fusion.ids_ref, f32[4,5]{1,0:T(4,128)} %w_ref.7, bf16[4,2,16,256,256]{4,3,2,1,0:T(8,128)(2,1)} %last_ref.3, ...), custom_call_target="tpu_custom_call" | custom-call | tf_op jit(solution)/shard_map/pallas_call | solution.py:117
  115.1 6.1 %shard_map.76 = (bf16[6,4,2,16,256]{4,3,2,1,0:T(8,128)(2,1)}, f32[6,4,2,16,256]{4,3,2,1,0:T(8,128)}) custom-call(s32[4]{0:T(128)} %ms_ref.7, s32[128]{0:T(128)} %li_ref.7, s32[2]{0:T(128)} %pad_add_fusion.ids_ref, f32[4,5]{1,0:T(4,128)} %w_ref.7, bf16[4,2,256,256]{3,2,1,0:T(8,128)(2,1)} %copy-done.1, bf16[4,2,256,256]{3,2,1,0:T(8,128)(2,1)} %copy-done, ...), custom_call_target="tpu_custom_call" | custom-call | tf_op jit(solution)/shard_map/pallas_call | solution.py:221
  127.6 3.3 %collective-permute-start.25 = (bf16[18,2,16,256]{3,2,0,1:T(8,128)(2,1)S(1)}, bf16[18,2,16,256]{3,2,0,1:T(8,128)(2,1)S(1)}, u32[]{:S(2)}, u32[]{:S(2)}) collective-permute-start(bf16[18,2,16,256]{3,2,0,1:T(8,128)(2,1)S(1)} %get-tuple-element.32), channel_id=1, source_target_pairs={{0,8},{1,9},{2,10},{3,11},{4,12},{5,13},{6,14},{7,15},{8,0},{9,1},... | collective-permute-start | bytes 884744 | tf_op jit(solution)/shard_map/ppermute | solution.py:27
  137.1 2.2 %collective-permute-start.32 = (bf16[18,2,16,256]{3,2,1,0:T(8,128)(2,1)S(1)}, bf16[18,2,16,256]{3,2,1,0:T(8,128)(2,1)S(1)}, u32[]{:S(2)}, u32[]{:S(2)}) collective-permute-start(bf16[18,2,16,256]{3,2,1,0:T(8,128)(2,1)S(1)} %get-tuple-element.36), channel_id=1, source_target_pairs={{0,12},{1,13},{2,14},{3,15},{4,0},{5,1},{6,2},{7,3},{8,4},{9,5},{1... | collective-permute-start | bytes 884744 | tf_op jit(solution)/shard_map/ppermute | solution.py:27
  139.4 5.8 %collective-permute-done.25 = bf16[18,2,16,256]{3,2,0,1:T(8,128)(2,1)S(1)} collective-permute-done((bf16[18,2,16,256]{3,2,0,1:T(8,128)(2,1)S(1)}, bf16[18,2,16,256]{3,2,0,1:T(8,128)(2,1)S(1)}, u32[]{:S(2)}, u32[]{:S(2)}) %collective-permute-start.25) | collective-permute-done | bytes 294944 | tf_op jit(solution)/shard_map/ppermute | solution.py:27
  145.4 3.0 %collective-permute-start.26 = (bf16[18,16,256]{2,1,0:T(8,128)(2,1)S(1)}, bf16[18,16,256]{2,1,0:T(8,128)(2,1)S(1)}, u32[]{:S(2)}, u32[]{:S(2)}) collective-permute-start(bf16[18,16,256]{2,1,0:T(8,128)(2,1)S(1)} %fusion.8), channel_id=1, source_target_pairs={{0,2},{1,3},{2,0},{3,1},{4,6},{5,7},{6,4},{7,5},{8,10},{9,11},{10,... | collective-permute-start | bytes 442376 | tf_op jit(solution)/shard_map/ppermute | solution.py:27
  149.8 7.2 %collective-permute-done.33 = bf16[18,2,16,256]{3,2,1,0:T(8,128)(2,1)S(1)} collective-permute-done((bf16[18,2,16,256]{3,2,1,0:T(8,128)(2,1)S(1)}, bf16[18,2,16,256]{3,2,1,0:T(8,128)(2,1)S(1)}, u32[]{:S(2)}, u32[]{:S(2)}) %collective-permute-start.33) | collective-permute-done | bytes 294944 | tf_op jit(solution)/shard_map/ppermute | solution.py:27
  157.2 4.5 %collective-permute-start.27 = (f32[16,256]{1,0:T(8,128)S(1)}, f32[16,256]{1,0:T(8,128)S(1)}, u32[]{:S(2)}, u32[]{:S(2)}) collective-permute-start(f32[16,256]{1,0:T(8,128)S(1)} %get-tuple-element.41), channel_id=1, source_target_pairs={{0,16},{16,32},{32,48},{48,64},{64,80},{80,96},{96,112},{1,17},{17... | collective-permute-start | bytes 49160 | tf_op jit(solution)/shard_map/ppermute | solution.py:31
  163.1 3.1 %collective-permute-start.34 = (bf16[18,16,256]{2,1,0:T(8,128)(2,1)S(1)}, bf16[18,16,256]{2,1,0:T(8,128)(2,1)S(1)}, u32[]{:S(2)}, u32[]{:S(2)}) collective-permute-start(bf16[18,16,256]{2,1,0:T(8,128)(2,1)S(1)} %fusion.9), channel_id=1, source_target_pairs={{0,2},{1,3},{2,0},{3,1},{4,6},{5,7},{6,4},{7,5},{8,10},{9,11},{10,... | collective-permute-start | bytes 442376 | tf_op jit(solution)/shard_map/ppermute | solution.py:27
  169.9 5.3 %collective-permute-start.35 = (f32[16,256]{1,0:T(8,128)S(1)}, f32[16,256]{1,0:T(8,128)S(1)}, u32[]{:S(2)}, u32[]{:S(2)}) collective-permute-start(f32[16,256]{1,0:T(8,128)S(1)} %get-tuple-element.45), channel_id=1, source_target_pairs={{0,16},{16,32},{32,48},{48,64},{64,80},{80,96},{96,112},{1,17},{17... | collective-permute-start | bytes 49160 | tf_op jit(solution)/shard_map/ppermute | solution.py:31
  176.6 5.1 %collective-permute-done.36 = f32[16,256]{1,0:T(8,128)S(1)} collective-permute-done((f32[16,256]{1,0:T(8,128)S(1)}, f32[16,256]{1,0:T(8,128)S(1)}, u32[]{:S(2)}, u32[]{:S(2)}) %collective-permute-start.36) | collective-permute-done | bytes 16416 | tf_op jit(solution)/shard_map/ppermute | solution.py:31
  (135 shorter events, 39.9 us)
Async XLA Ops:
  0.7 10.4 %collective-permute-start.12 = (bf16[2,16,256]{2,1,0:T(8,128)(2,1)S(1)}, bf16[2,16,256]{2,1,0:T(8,128)(2,1)S(1)}, u32[]{:S(2)}, u32[]{:S(2)}) collective-permute-start(bf16[2,16,256]{2,1,0:T(8,128)(2,1)S(1)} %get-tuple-element.49), channel_id=1, source_target_pairs={{0,16},{16,32},{32,48},{48,64},{64,80},{80,96},{96,112},{1,17},{17... | collective-permute-start | bytes 49160 | tf_op jit(solution)/shard_map/ppermute | solution.py:31
  6.6 14.1 %collective-permute-start.11 = (bf16[16,16,256]{2,1,0:T(8,128)(2,1)S(1)}, bf16[16,16,256]{2,1,0:T(8,128)(2,1)S(1)}, u32[]{:S(2)}, u32[]{:S(2)}) collective-permute-start(bf16[16,16,256]{2,1,0:T(8,128)(2,1)S(1)} %get-tuple-element.48), channel_id=1, source_target_pairs={{0,2},{1,3},{2,0},{3,1},{4,6},{5,7},{6,4},{7,5},{8,10},{9,11},{10,... | collective-permute-start | bytes 393224 | tf_op jit(solution)/shard_map/ppermute | solution.py:27
  11.2 11.0 %collective-permute-start.14 = (bf16[4,16,256]{2,1,0:T(8,128)(2,1)S(1)}, bf16[4,16,256]{2,1,0:T(8,128)(2,1)S(1)}, u32[]{:S(2)}, u32[]{:S(2)}) collective-permute-start(bf16[4,16,256]{2,1,0:T(8,128)(2,1)S(1)} %pad_maximum_fusion.4), channel_id=1, source_target_pairs={{0,2},{1,3},{2,0},{3,1},{4,6},{5,7},{6,4},{7,5},{8,10},{9,11},{10,... | collective-permute-start | bytes 98312 | tf_op jit(solution)/shard_map/ppermute | solution.py:27
  16.5 10.3 %collective-permute-start.3 = (bf16[32,16,256]{2,1,0:T(8,128)(2,1)S(1)}, bf16[32,16,256]{2,1,0:T(8,128)(2,1)S(1)}, u32[]{:S(2)}, u32[]{:S(2)}) collective-permute-start(bf16[32,16,256]{2,1,0:T(8,128)(2,1)S(1)} %pad_maximum_fusion.3.rest_0_), channel_id=1, source_target_pairs={{0,4},{1,5},{2,6},{3,7},{4,8},{5,9},{6,10},{7,11},{8,12},{9,13},{1... | collective-permute-start | bytes 786440 | tf_op jit(solution)/shard_map/ppermute | solution.py:27
  18.0 15.0 %collective-permute-start.2 = (bf16[32,16,256]{2,1,0:T(8,128)(2,1)S(1)}, bf16[32,16,256]{2,1,0:T(8,128)(2,1)S(1)}, u32[]{:S(2)}, u32[]{:S(2)}) collective-permute-start(bf16[32,16,256]{2,1,0:T(8,128)(2,1)S(1)} %pad_maximum_fusion.3.rest_0_), channel_id=1, source_target_pairs={{0,8},{1,9},{2,10},{3,11},{4,12},{5,13},{6,14},{7,15},{8,0},{9,1},... | collective-permute-start | bytes 786440 | tf_op jit(solution)/shard_map/ppermute | solution.py:27
  20.8 12.2 %collective-permute-start.1 = (bf16[32,16,256]{2,1,0:T(8,128)(2,1)S(1)}, bf16[32,16,256]{2,1,0:T(8,128)(2,1)S(1)}, u32[]{:S(2)}, u32[]{:S(2)}) collective-permute-start(bf16[32,16,256]{2,1,0:T(8,128)(2,1)S(1)} %pad_maximum_fusion.3.rest_0_), channel_id=1, source_target_pairs={{0,12},{1,13},{2,14},{3,15},{4,0},{5,1},{6,2},{7,3},{8,4},{9,5},{1... | collective-permute-start | bytes 786440 | tf_op jit(solution)/shard_map/ppermute | solution.py:27
  22.3 13.4 %collective-permute-start.18 = (bf16[40,16,256]{2,1,0:T(8,128)(2,1)S(1)}, bf16[40,16,256]{2,1,0:T(8,128)(2,1)S(1)}, u32[]{:S(2)}, u32[]{:S(2)}) collective-permute-start(bf16[40,16,256]{2,1,0:T(8,128)(2,1)S(1)} %constant_dynamic-update-slice_fusion.rest_0_), channel_id=1, source_target_pairs={{0,1},{1,0},{2,3},{3,2},{4,5},{5,4},{6,7},{7,6},{8,9},{9,8},{10,11... | collective-permute-start | bytes 983048 | tf_op jit(solution)/shard_map/ppermute | solution.py:27
  25.4 56.8 %collective-permute-start.10 = (bf16[4,2,256,256]{3,2,1,0:T(8,128)(2,1)}, bf16[4,2,256,256]{3,2,1,0:T(8,128)(2,1)S(1)}, u32[]{:S(2)}, u32[]{:S(2)}) collective-permute-start(bf16[4,2,256,256]{3,2,1,0:T(8,128)(2,1)} %get-tuple-element.25), channel_id=1, source_target_pairs={{16,0},{32,16},{48,32},{64,48},{80,64},{96,80},{112,96},{17,1},{33... | collective-permute-start | bytes 3145736 | tf_op jit(solution)/shard_map/ppermute | solution.py:31
  26.8 55.5 %collective-permute-start.9 = (bf16[4,2,256,256]{3,2,1,0:T(8,128)(2,1)}, bf16[4,2,256,256]{3,2,1,0:T(8,128)(2,1)S(1)}, u32[]{:S(2)}, u32[]{:S(2)}) collective-permute-start(bf16[4,2,256,256]{3,2,1,0:T(8,128)(2,1)} %get-tuple-element.26), channel_id=1, source_target_pairs={{0,16},{16,32},{32,48},{48,64},{64,80},{80,96},{96,112},{1,17},{17... | collective-permute-start | bytes 3145736 | tf_op jit(solution)/shard_map/ppermute | solution.py:31
  33.0 17.4 %collective-permute-start.17 = (bf16[40,16,256]{2,1,0:T(8,128)(2,1)S(1)}, bf16[40,16,256]{2,1,0:T(8,128)(2,1)S(1)}, u32[]{:S(2)}, u32[]{:S(2)}) collective-permute-start(bf16[40,16,256]{2,1,0:T(8,128)(2,1)S(1)} %constant_dynamic-update-slice_fusion.rest_0_), channel_id=1, source_target_pairs={{0,4},{1,5},{2,6},{3,7},{4,8},{5,9},{6,10},{7,11},{8,12},{9,13},{1... | collective-permute-start | bytes 983048 | tf_op jit(solution)/shard_map/ppermute | solution.py:27
  33.0 17.4 %collective-permute-start.16 = (bf16[40,16,256]{2,1,0:T(8,128)(2,1)S(1)}, bf16[40,16,256]{2,1,0:T(8,128)(2,1)S(1)}, u32[]{:S(2)}, u32[]{:S(2)}) collective-permute-start(bf16[40,16,256]{2,1,0:T(8,128)(2,1)S(1)} %constant_dynamic-update-slice_fusion.rest_0_), channel_id=1, source_target_pairs={{0,8},{1,9},{2,10},{3,11},{4,12},{5,13},{6,14},{7,15},{8,0},{9,1},... | collective-permute-start | bytes 983048 | tf_op jit(solution)/shard_map/ppermute | solution.py:27
  35.7 15.5 %collective-permute-start.15 = (bf16[40,16,256]{2,1,0:T(8,128)(2,1)S(1)}, bf16[40,16,256]{2,1,0:T(8,128)(2,1)}, u32[]{:S(2)}, u32[]{:S(2)}) collective-permute-start(bf16[40,16,256]{2,1,0:T(8,128)(2,1)S(1)} %constant_dynamic-update-slice_fusion.rest_0_), channel_id=1, source_target_pairs={{0,12},{1,13},{2,14},{3,15},{4,0},{5,1},{6,2},{7,3},{8,4},{9,5},{1... | collective-permute-start | bytes 983048 | tf_op jit(solution)/shard_map/ppermute | solution.py:27
  51.9 30.2 %collective-permute-start.21 = (bf16[40,16,256]{2,1,0:T(8,128)(2,1)S(1)}, bf16[40,16,256]{2,1,0:T(8,128)(2,1)S(1)}, u32[]{:S(2)}, u32[]{:S(2)}) collective-permute-start(bf16[40,16,256]{2,1,0:T(8,128)(2,1)S(1)} %collective-permute-done.17.rest_3_), channel_id=1, source_target_pairs={{0,1},{1,0},{2,3},{3,2},{4,5},{5,4},{6,7},{7,6},{8,9},{9,8},{10,11... | collective-permute-start | bytes 983048 | tf_op jit(solution)/shard_map/ppermute | solution.py:27
  52.3 29.9 %collective-permute-start.20 = (bf16[40,16,256]{2,1,0:T(8,128)(2,1)S(1)}, bf16[40,16,256]{2,1,0:T(8,128)(2,1)}, u32[]{:S(2)}, u32[]{:S(2)}) collective-permute-start(bf16[40,16,256]{2,1,0:T(8,128)(2,1)S(1)} %collective-permute-done.16.rest_2_), channel_id=1, source_target_pairs={{0,1},{1,0},{2,3},{3,2},{4,5},{5,4},{6,7},{7,6},{8,9},{9,8},{10,11... | collective-permute-start | bytes 983048 | tf_op jit(solution)/shard_map/ppermute | solution.py:27
  52.7 29.6 %collective-permute-start.19 = (bf16[40,16,256]{2,1,0:T(8,128)(2,1)}, bf16[40,16,256]{2,1,0:T(8,128)(2,1)}, u32[]{:S(2)}, u32[]{:S(2)}) collective-permute-start(bf16[40,16,256]{2,1,0:T(8,128)(2,1)} %collective-permute-done.15.rest_1_), channel_id=1, source_target_pairs={{0,1},{1,0},{2,3},{3,2},{4,5},{5,4},{6,7},{7,6},{8,9},{9,8},{10,11... | collective-permute-start | bytes 983048 | tf_op jit(solution)/shard_map/ppermute | solution.py:27
  82.2 42.4 %collective-permute-start.8 = (bf16[16,4,2,16,256]{4,3,0,2,1:T(8,128)(2,1)}, bf16[16,4,2,16,256]{4,3,0,2,1:T(8,128)(2,1)}, u32[]{:S(2)}, u32[]{:S(2)}) collective-permute-start(bf16[16,4,2,16,256]{4,3,0,2,1:T(8,128)(2,1)} %copy.9), channel_id=1, source_target_pairs={{0,1},{1,0},{2,3},{3,2},{4,5},{5,4},{6,7},{7,6},{8,9},{9,8},{10,11... | collective-permute-start | bytes 3145736 | tf_op jit(solution)/shard_map/ppermute | solution.py:27
  90.6 31.2 %collective-permute-start.22 = (bf16[6,4,2,16,256]{4,3,0,2,1:T(8,128)(2,1)S(1)}, bf16[6,4,2,16,256]{4,3,0,2,1:T(8,128)(2,1)S(1)}, u32[]{:S(2)}, u32[]{:S(2)}) collective-permute-start(bf16[6,4,2,16,256]{4,3,0,2,1:T(8,128)(2,1)S(1)} %copy.15), channel_id=1, source_target_pairs={{0,1},{1,0},{2,3},{3,2},{4,5},{5,4},{6,7},{7,6},{8,9},{9,8},{10,11... | collective-permute-start | bytes 1179656 | tf_op jit(solution)/shard_map/ppermute | solution.py:27
  126.8 10.3 %collective-permute-start.23 = (bf16[18,2,16,256]{3,2,0,1:T(8,128)(2,1)S(1)}, bf16[18,2,16,256]{3,2,0,1:T(8,128)(2,1)S(1)}, u32[]{:S(2)}, u32[]{:S(2)}) collective-permute-start(bf16[18,2,16,256]{3,2,0,1:T(8,128)(2,1)S(1)} %get-tuple-element.31), channel_id=1, source_target_pairs={{0,4},{1,5},{2,6},{3,7},{4,8},{5,9},{6,10},{7,11},{8,12},{9,13},{1... | collective-permute-start | bytes 884744 | tf_op jit(solution)/shard_map/ppermute | solution.py:27
  127.6 17.5 %collective-permute-start.25 = (bf16[18,2,16,256]{3,2,0,1:T(8,128)(2,1)S(1)}, bf16[18,2,16,256]{3,2,0,1:T(8,128)(2,1)S(1)}, u32[]{:S(2)}, u32[]{:S(2)}) collective-permute-start(bf16[18,2,16,256]{3,2,0,1:T(8,128)(2,1)S(1)} %get-tuple-element.32), channel_id=1, source_target_pairs={{0,8},{1,9},{2,10},{3,11},{4,12},{5,13},{6,14},{7,15},{8,0},{9,1},... | collective-permute-start | bytes 884744 | tf_op jit(solution)/shard_map/ppermute | solution.py:27
  130.9 14.2 %collective-permute-start.24 = (bf16[18,2,16,256]{3,2,0,1:T(8,128)(2,1)S(1)}, bf16[18,2,16,256]{3,2,0,1:T(8,128)(2,1)S(1)}, u32[]{:S(2)}, u32[]{:S(2)}) collective-permute-start(bf16[18,2,16,256]{3,2,0,1:T(8,128)(2,1)S(1)} %get-tuple-element.33), channel_id=1, source_target_pairs={{0,12},{1,13},{2,14},{3,15},{4,0},{5,1},{6,2},{7,3},{8,4},{9,5},{1... | collective-permute-start | bytes 884744 | tf_op jit(solution)/shard_map/ppermute | solution.py:27
  133.7 16.1 %collective-permute-start.31 = (bf16[18,2,16,256]{3,2,1,0:T(8,128)(2,1)S(1)}, bf16[18,2,16,256]{3,2,1,0:T(8,128)(2,1)S(1)}, u32[]{:S(2)}, u32[]{:S(2)}) collective-permute-start(bf16[18,2,16,256]{3,2,1,0:T(8,128)(2,1)S(1)} %get-tuple-element.34), channel_id=1, source_target_pairs={{0,4},{1,5},{2,6},{3,7},{4,8},{5,9},{6,10},{7,11},{8,12},{9,13},{1... | collective-permute-start | bytes 884744 | tf_op jit(solution)/shard_map/ppermute | solution.py:27
  134.4 22.6 %collective-permute-start.33 = (bf16[18,2,16,256]{3,2,1,0:T(8,128)(2,1)S(1)}, bf16[18,2,16,256]{3,2,1,0:T(8,128)(2,1)S(1)}, u32[]{:S(2)}, u32[]{:S(2)}) collective-permute-start(bf16[18,2,16,256]{3,2,1,0:T(8,128)(2,1)S(1)} %get-tuple-element.35), channel_id=1, source_target_pairs={{0,8},{1,9},{2,10},{3,11},{4,12},{5,13},{6,14},{7,15},{8,0},{9,1},... | collective-permute-start | bytes 884744 | tf_op jit(solution)/shard_map/ppermute | solution.py:27
  137.1 19.9 %collective-permute-start.32 = (bf16[18,2,16,256]{3,2,1,0:T(8,128)(2,1)S(1)}, bf16[18,2,16,256]{3,2,1,0:T(8,128)(2,1)S(1)}, u32[]{:S(2)}, u32[]{:S(2)}) collective-permute-start(bf16[18,2,16,256]{3,2,1,0:T(8,128)(2,1)S(1)} %get-tuple-element.36), channel_id=1, source_target_pairs={{0,12},{1,13},{2,14},{3,15},{4,0},{5,1},{6,2},{7,3},{8,4},{9,5},{1... | collective-permute-start | bytes 884744 | tf_op jit(solution)/shard_map/ppermute | solution.py:27
  145.4 11.8 %collective-permute-start.26 = (bf16[18,16,256]{2,1,0:T(8,128)(2,1)S(1)}, bf16[18,16,256]{2,1,0:T(8,128)(2,1)S(1)}, u32[]{:S(2)}, u32[]{:S(2)}) collective-permute-start(bf16[18,16,256]{2,1,0:T(8,128)(2,1)S(1)} %fusion.8), channel_id=1, source_target_pairs={{0,2},{1,3},{2,0},{3,1},{4,6},{5,7},{6,4},{7,5},{8,10},{9,11},{10,... | collective-permute-start | bytes 442376 | tf_op jit(solution)/shard_map/ppermute | solution.py:27
  (32 other events, 315.2 us)

commit v2 on v1

v2 whole, which is shorter than its diff:
```python
import functools

import jax
import jax.numpy as jnp
from jax import lax
from jax.experimental import pallas as pl
from jax.experimental.pallas import tpu as pltpu
from jax.sharding import PartitionSpec as P


NXC, NH, NC = 4, 2, 2
BF = jnp.bfloat16
F32 = jnp.float32


def pairs_of(dx, dh, dc):
    out = []
    for x in range(NXC):
        for h in range(NH):
            for c in range(NC):
                dest = ((x + dx) % NXC) * 4 + ((h + dh) % NH) * 2 + (c + dc) % NC
                out.append((x * 4 + h * 2 + c, dest))
    return out


def move(value, dx=0, dh=0, dc=0):
    return lax.ppermute(value, "mem", pairs_of(dx, dh, dc))


def shift(value, pairs):
    return lax.ppermute(value, "lev", pairs)


def rows_at(mem, j, hr, cr):
    x = mem // 4
    h = (mem // 2) % 2
    c = mem % 2
    block = ((x + j) % 4) * 4 + ((h + hr) % 2) * 2 + (c + cr) % 2
    return pl.multiple_of(block * 16, 16)


def field(p, g, ky, kx):
    product = p * g
    rows = jnp.dot(ky, product, preferred_element_type=F32).astype(BF)
    smoothed = lax.dot_general(
        rows, kx, (((1,), (1,)), ((), ())), preferred_element_type=F32
    )
    return smoothed.astype(BF)


def own_kernel(
    ms_ref, li_ref, ids_ref, w_ref, p_ref, q_ref, ky_ref, kx_ref, *rest, levels, inv
):
    pieces = rest[:8]
    send_ref, keep_ref, gs, acc, *rings = rest[8:]
    t = pl.program_id(0)
    mem = ids_ref[0]
    base = ids_ref[1] * levels

    @pl.when(t == 0)
    def _():
        for ring in rings:
            for slot in (3, 4):
                ring[slot] = jnp.zeros(ring.shape[1:], F32)

    lo = t - 2
    level = jnp.minimum(t, levels - 1)
    newest = lax.rem(t, 5)
    slots = [lax.rem(t + 1 + d, 5) for d in range(5)]

    def coef(k, d):
        other = lo + d
        a = jnp.clip(base + lo, 0, 127)
        b = jnp.clip(base + other, 0, 127)
        ok = (other >= 0) & (other < levels) & (li_ref[a] == li_ref[b])
        return jnp.where(ok, w_ref[ms_ref[k], d + 2], 0.0) * inv

    for cr in range(2):
        for hr in range(2):
            for j in range(4):
                block = pieces[cr * 4 + j][hr * levels + level]
                gs[pl.ds(rows_at(mem, j, hr, cr), 16), :] = block
    g = gs[...]

    for k in range(4):
        s = ms_ref[k]
        rings[k][newest] = field(p_ref[k, 0, 0], g, ky_ref[s], kx_ref[s]).astype(F32)
        cs = [coef(k, d) for d in range(-2, 3)]
        for cr in range(2):
            for hr in range(2):
                for j in range(4):
                    place = cr * 8 + hr * 4 + j
                    r0 = rows_at(mem, j, hr, cr)
                    mix = None
                    for d in range(5):
                        term = cs[d] * rings[k][slots[d], pl.ds(r0, 16), :]
                        mix = term if mix is None else mix + term
                    mix = mix * q_ref[k, 0, 0, pl.ds(r0, 16), :].astype(F32)
                    if k:
                        mix = mix + acc[place]
                    if k < 3:
                        acc[place] = mix
                    elif cr:
                        send_ref[j, hr, 0] = mix.astype(BF)
                    else:
                        keep_ref[j, hr, 0] = mix


def own_part(v, ms, li, ids, w, p, ky, kx, pieces, inv):
    levels = p.shape[2]
    smem = pl.BlockSpec(memory_space=pltpu.SMEM)
    whole = pl.BlockSpec((4, 256, 256), lambda t, *_: (0, 0, 0))
    pblock = (4, 1, 1, 256, 256)
    part = pl.BlockSpec((4, 2, 1, 16, 256), lambda t, *_: (0, 0, jnp.maximum(t - 2, 0), 0, 0))
    return pl.pallas_call(
        functools.partial(own_kernel, levels=levels, inv=inv),
        grid_spec=pltpu.PrefetchScalarGridSpec(
            num_scalar_prefetch=3,
            grid=(levels + 2,),
            in_specs=[
                smem,
                pl.BlockSpec(pblock, lambda t, *_: (0, v, jnp.minimum(t, levels - 1), 0, 0)),
                pl.BlockSpec(pblock, lambda t, *_: (0, v, jnp.maximum(t - 2, 0), 0, 0)),
                whole,
                whole,
            ]
            + [pl.BlockSpec((2 * levels, 16, 256), lambda t, *_: (0, 0, 0))] * 8,
            out_specs=[part, part],
            scratch_shapes=[
                pltpu.VMEM((256, 256), BF),
                pltpu.VMEM((16, 16, 256), F32),
            ]
            + [pltpu.VMEM((5, 256, 256), F32)] * 4,
        ),
        out_shape=[
            jax.ShapeDtypeStruct((4, 2, levels, 16, 256), BF),
            jax.ShapeDtypeStruct((4, 2, levels, 16, 256), F32),
        ],
    )(ms, li, ids, w, p, p, ky, kx, *pieces)


def edge_kernel(
    ms_ref, li_ref, ids_ref, w_ref, above_ref, below_ref, first_ref, last_ref, ky_ref, kx_ref,
    *rest, v, levels, inv
):
    pieces, lasts = rest[:8], rest[8:16]
    send_ref, keep_ref, gs, hs = rest[16:]
    mem = ids_ref[0]
    base = ids_ref[1] * levels
    for side in range(2):
        top = side == 0
        halo_ref = above_ref if top else below_ref
        p_ref = first_ref if top else last_ref
        level = 1 if top else levels - 2
        for cr in range(2):
            for j in range(4):
                last, piece = lasts[cr * 4 + j], pieces[cr * 4 + j]
                for hr in range(2):
                    rows = pl.ds(rows_at(mem, j, hr, cr), 16)
                    gs[2 * side, rows, :] = last[(4 - 4 * hr) + side * 2 + v]
                    gs[2 * side + 1, rows, :] = piece[hr * levels + level]
        for k in range(4):
            s = ms_ref[k]
            hs[2 * side, k] = field(halo_ref[k, 0], gs[2 * side], ky_ref[s], kx_ref[s])
            hs[2 * side + 1, k] = field(
                p_ref[k, 0, 1 if top else 0], gs[2 * side + 1], ky_ref[s], kx_ref[s]
            )
    for side in range(2):
        top = side == 0
        halo_ref = above_ref if top else below_ref
        p_ref = first_ref if top else last_ref
        far = base - 1 if top else base + levels
        near = base if top else base + levels - 1
        after = base + 1 if top else base + levels - 2
        inside = (far >= 0) & (far < 128)
        far_id = li_ref[jnp.clip(far, 0, 127)]
        ok1 = inside & (far_id == li_ref[near])
        ok2 = inside & (far_id == li_ref[after])

        def pick(k, place, ok):
            return jnp.where(ok, w_ref[ms_ref[k], place], 0.0) * inv

        c_near = [pick(k, 1 if top else 3, ok1) for k in range(4)]
        c_next = [pick(k, 0 if top else 4, ok2) for k in range(4)]
        c_back = [pick(k, 4 if top else 0, ok2) for k in range(4)]
        i_near = 0 if top else 1
        for cr in range(2):
            for j in range(4):
                for hr in range(2):
                    rows = pl.ds(rows_at(mem, j, hr, cr), 16)
                    a, b, e = None, None, None
                    for k in range(4):
                        h = hs[2 * side, k, rows, :].astype(F32)
                        a_k = c_near[k] * (h * p_ref[k, 0, i_near, rows, :].astype(F32))
                        b_k = c_next[k] * (h * p_ref[k, 0, 1 - i_near, rows, :].astype(F32))
                        e_k = c_back[k] * (
                            hs[2 * side + 1, k, rows, :].astype(F32)
                            * halo_ref[k, 0, rows, :].astype(F32)
                        )
                        a = a_k if a is None else a + a_k
                        b = b_k if b is None else b + b_k
                        e = e_k if e is None else e + e_k
                    places = (0, 1) if top else (3, 2)
                    for n, value in zip((*places, 4 + side), (a, b, e)):
                        if cr:
                            send_ref[j, hr, n] = value.astype(BF)
                        else:
                            keep_ref[j, hr, n] = value


def edge_part(v, ms, li, ids, w, above, below, p, ky, kx, pieces, lasts, inv):
    levels = p.shape[2]
    smem = pl.BlockSpec(memory_space=pltpu.SMEM)
    whole = pl.BlockSpec((4, 256, 256), lambda t, *_: (0, 0, 0))
    halo = pl.BlockSpec((4, 1, 256, 256), lambda t, *_: (0, v, 0, 0))
    part = pl.BlockSpec((4, 2, 6, 16, 256), lambda t, *_: (0, 0, 0, 0, 0))
    return pl.pallas_call(
        functools.partial(edge_kernel, v=v, levels=levels, inv=inv),
        grid_spec=pltpu.PrefetchScalarGridSpec(
            num_scalar_prefetch=3,
            grid=(1,),
            in_specs=[
                smem,
                halo,
                halo,
                pl.BlockSpec((4, 1, 2, 256, 256), lambda t, *_: (0, v, 0, 0, 0)),
                pl.BlockSpec((4, 1, 2, 256, 256), lambda t, *_: (0, v, levels // 2 - 1, 0, 0)),
                whole,
                whole,
            ]
            + [pl.BlockSpec((2 * levels, 16, 256), lambda t, *_: (0, 0, 0))] * 8
            + [pl.BlockSpec((8, 16, 256), lambda t, *_: (2 * levels // 8, 0, 0))] * 8,
            out_specs=[part, part],
            scratch_shapes=[
                pltpu.VMEM((4, 256, 256), BF),
                pltpu.VMEM((4, 4, 256, 256), BF),
            ],
        ),
        out_shape=[
            jax.ShapeDtypeStruct((4, 2, 6, 16, 256), BF),
            jax.ShapeDtypeStruct((4, 2, 6, 16, 256), F32),
        ],
    )(ms, li, ids, w, above, below, p, p, ky, kx, *pieces, *lasts)


def gather_x(payload):
    got = {j: move(payload, dx=-j) for j in (1, 3, 2)}
    return [payload, got[1], got[2], got[3]]


def gather_c(pieces):
    return pieces + [move(piece, dc=1) for piece in pieces]


def scatter_rows(total):
    got = [move(total[j].astype(BF), dx=j) for j in (1, 3, 2)]
    mine = total[0]
    for piece in got:
        mine = mine + piece.astype(F32)
    return mine[0] + move(mine[1].astype(BF), dh=1).astype(F32)


def per_device(
    perturbations, gradient, member_scale, kernel_y, kernel_x, vertical_weights, layer_index
):
    levels = perturbations.shape[2]
    inv = 1.0 / (perturbations.shape[0] * lax.axis_size("mem") - 1)
    count = lax.axis_size("lev")
    up = [(i, i + 1) for i in range(count - 1)]
    down = [(i + 1, i) for i in range(count - 1)]
    ids = jnp.stack([lax.axis_index("mem"), lax.axis_index("lev")]).astype(jnp.int32)

    gh_up = shift(gradient[:, levels - 1], up)
    gh_down = shift(gradient[:, 0], down)
    other = move(gradient[0], dh=1)
    later = jnp.concatenate([gradient[1], gh_up, gh_down])
    other_later = move(later, dh=1)
    p_last, p_first = perturbations[:, :, levels - 1], perturbations[:, :, 0]
    above = shift(p_last, up)
    below = shift(p_first, down)
    x0 = gather_x(jnp.concatenate([gradient[0], other]))
    x1 = gather_x(jnp.concatenate([later[:levels], other_later, later[levels:]]))
    pieces = [gather_c(x0), gather_c(x1)]

    def own_sums(v):
        send, keep = own_part(
            v, member_scale, layer_index, ids, vertical_weights, perturbations,
            kernel_y, kernel_x, pieces[v], inv,
        )
        return keep + move(send, dc=1).astype(F32)

    def edge_sums(v):
        send, keep = edge_part(
            v, member_scale, layer_index, ids, vertical_weights, above, below,
            perturbations, kernel_y, kernel_x, pieces[v], pieces[1], inv,
        )
        return keep + move(send, dc=1).astype(F32)

    def joined(own, edge):
        return [
            own[:, :, :2] + edge[:, :, :2],
            own[:, :, 2 : levels - 2],
            own[:, :, levels - 2 :] + edge[:, :, 2:4],
        ]

    def closed(mine, from_above, from_below):
        return jnp.concatenate(
            [
                (mine[0] + from_above)[None],
                mine[1 : levels - 1],
                (mine[levels - 1] + from_below)[None],
            ]
        )

    own = own_sums(0)
    edges = [edge_sums(0), edge_sums(1)]
    later = lax.optimization_barrier(edges[1][:, :, :4])
    total = jnp.concatenate(
        joined(own, edges[0]) + [edges[0][:, :, 4:], edges[1][:, :, 4:]], axis=2
    )
    first = scatter_rows(total)
    backs = first[levels:].reshape((2, 2) + first.shape[1:])
    from_above = shift(backs[:, 1], up)
    from_below = shift(backs[:, 0], down)
    second = scatter_rows(jnp.concatenate(joined(own_sums(1), later), axis=2))
    return jnp.stack(
        [
            closed(first[:levels], from_above[0], from_below[0]),
            closed(second, from_above[1], from_below[1]),
        ]
    )


def solution(mesh):
    placed = (
        P("mem", None, "lev", None, None),
        P(None, "lev", "mem", None),
        P("mem"),
        P(),
        P(),
        P(),
        P(),
    )
    return jax.shard_map(
        per_device,
        mesh=mesh,
        in_specs=placed,
        out_specs=P(None, "lev", "mem", None),
        check_vma=False,
    )
```

time: 185 us -> 168 us (0.908)
  starting transfers between devices: 56.7 us -> 49.5 us
  local copies, waits for them, and re-layouts: 15 us -> 9.58 us
  waiting for transfers between devices: 44 us -> 40.2 us
    ppermute x8 -> x6, starting transfers between devices: 23.8 us -> 18.5 us  [shift(): return lax.ppermute(value, 'lev', pairs)]
    pallas_call x2 -> x0, local copies, waits for them, and re-layouts: 3.35 us -> none  [the longest x1 2.33 us: own_part(): pl.pallas_call(functools.partial(own_kernel, levels=levels, inv=inv), gri...]
    ppermute x29 -> x28, waiting for transfers between devices: 36.9 us -> 33.8 us  [move(): return lax.ppermute(value, 'mem', pairs_of(dx, dh, dc))]
    unnamed x43 -> x46, local copies, waits for them, and re-layouts: 6.27 us -> 3.53 us
    ppermute x29 -> x28, starting transfers between devices: 32.9 us -> 31 us  [move(): return lax.ppermute(value, 'mem', pairs_of(dx, dh, dc))]
    ppermute x8 -> x6, waiting for transfers between devices: 7.15 us -> 6.47 us  [shift(): return lax.ppermute(value, 'lev', pairs)]
    squeeze x5 -> x4, local copies, waits for them, and re-layouts: 4.81 us -> 4.78 us  [the longest x1 3.05 us: per_device(): p_last, p_first = (perturbations[:, :, levels - 1], perturbations[:, :, 0])]
  transfers between devices with their start and end apart: 37 -> 34, of which waited for: 16 -> 14; matrix products, arithmetic and copies ran while one was open for 9% -> 5% of each run, Pallas kernels for 33% -> 37%
where the time goes in v2:
time: 168 us; the launch traced here: 165 us
  Pallas kernels  60.7 us (36%)
  starting transfers between devices  49.5 us (29%)
  waiting for transfers between devices  40.2 us (24%)
  local copies, waits for them, and re-layouts  9.58 us (6%)
  other arithmetic  4.88 us (3%)
    pallas_call x2, Pallas kernels, own_part(): pl.pallas_call(functools.partial(own_kernel, levels=levels, inv=inv), gri...  47.2 us
    ppermute x28, waiting for transfers between devices, move(): return lax.ppermute(value, 'mem', pairs_of(dx, dh, dc))  33.8 us
    ppermute x28, starting transfers between devices, move(): return lax.ppermute(value, 'mem', pairs_of(dx, dh, dc))  31 us
    ppermute x6, starting transfers between devices, shift(): return lax.ppermute(value, 'lev', pairs)  18.5 us
    pallas_call x2, Pallas kernels, edge_part(): pl.pallas_call(functools.partial(edge_kernel, v=v, levels=levels, inv=inv...  13.5 us
    ppermute x6, waiting for transfers between devices, shift(): return lax.ppermute(value, 'lev', pairs)  6.47 us
    unnamed x46, local copies, waits for them, and re-layouts  3.53 us
  transfers between devices with their start and end apart: 34, of which 14 were waited for; matrix products, arithmetic and copies ran while one was open for 5% of the time, Pallas kernels for 37%

profile of v2, /device:TPU:0, one launch (start us, length us, event | category | flops | bytes accessed | tf_op | source)
XLA Modules:
  0.0 165.5 jit_solution(4942539809829053075)
XLA Ops:
  0.7 3.6 %collective-permute-start.11 = (bf16[2,16,256]{2,1,0:T(8,128)(2,1)S(1)}, bf16[2,16,256]{2,1,0:T(8,128)(2,1)S(1)}, u32[]{:S(2)}, u32[]{:S(2)}) collective-permute-start(bf16[2,16,256]{2,1,0:T(8,128)(2,1)S(1)} %get-tuple-element.37), channel_id=1, source_target_pairs={{0,16},{16,32},{32,48},{48,64},{64,80},{80,96},{96,112},{1,17},{17... | collective-permute-start | bytes 49160 | tf_op jit(solution)/shard_map/ppermute | solution.py:31
  6.6 3.0 %collective-permute-start = (bf16[16,16,256]{2,1,0:T(8,128)(2,1)S(1)}, bf16[16,16,256]{2,1,0:T(8,128)(2,1)S(1)}, u32[]{:S(2)}, u32[]{:S(2)}) collective-permute-start(bf16[16,16,256]{2,1,0:T(8,128)(2,1)S(1)} %get-tuple-element.36), channel_id=1, source_target_pairs={{0,2},{1,3},{2,0},{3,1},{4,6},{5,7},{6,4},{7,5},{8,10},{9,11},{10,... | collective-permute-start | bytes 393224 | tf_op jit(solution)/shard_map/ppermute | solution.py:27
  10.0 3.1 %collective-permute-start.13 = (bf16[20,16,256]{2,1,0:T(8,128)(2,1)S(1)}, bf16[20,16,256]{2,1,0:T(8,128)(2,1)S(1)}, u32[]{:S(2)}, u32[]{:S(2)}) collective-permute-start(bf16[20,16,256]{2,1,0:T(8,128)(2,1)S(1)} %pad_maximum_fusion.4), channel_id=1, source_target_pairs={{0,2},{1,3},{2,0},{3,1},{4,6},{5,7},{6,4},{7,5},{8,10},{9,11},{10,... | collective-permute-start | bytes 491528 | tf_op jit(solution)/shard_map/ppermute | solution.py:27
  13.4 1.6 collective-permute-start.3
  14.9 2.7 %collective-permute-start.2 = (bf16[32,16,256]{2,1,0:T(8,128)(2,1)S(1)}, bf16[32,16,256]{2,1,0:T(8,128)(2,1)S(1)}, u32[]{:S(2)}, u32[]{:S(2)}) collective-permute-start(bf16[32,16,256]{2,1,0:T(8,128)(2,1)S(1)} %pad_maximum_fusion.3.rest_0_), channel_id=1, source_target_pairs={{0,8},{1,9},{2,10},{3,11},{4,12},{5,13},{6,14},{7,15},{8,0},{9,1},... | collective-permute-start | bytes 786440 | tf_op jit(solution)/shard_map/ppermute | solution.py:27
  19.3 3.0 %slice_bitcast_fusion = (bf16[4,2,256,256]{3,2,1,0:T(8,128)(2,1)}, bf16[4,2,256,256]{3,2,1,0:T(8,128)(2,1)}) fusion(bf16[4,2,16,256,256]{4,3,2,1,0:T(8,128)(2,1)} %q_ref.3), kind=kLoop, calls=%fused_computation.4 | loop fusion | bytes 4194304 | tf_op jit(solution)/shard_map/squeeze | solution.py:278
  23.7 6.6 %collective-permute-start.9 = (bf16[4,2,256,256]{3,2,1,0:T(8,128)(2,1)}, bf16[4,2,256,256]{3,2,1,0:T(8,128)(2,1)}, u32[]{:S(2)}, u32[]{:S(2)}) collective-permute-start(bf16[4,2,256,256]{3,2,1,0:T(8,128)(2,1)} %get-tuple-element.22), channel_id=1, source_target_pairs={{0,16},{16,32},{32,48},{48,64},{64,80},{80,96},{96,112},{1,17},{17... | collective-permute-start | bytes 3145736 | tf_op jit(solution)/shard_map/ppermute | solution.py:31
  30.9 2.0 %collective-permute-start.15 = (bf16[40,16,256]{2,1,0:T(8,128)(2,1)S(1)}, bf16[40,16,256]{2,1,0:T(8,128)(2,1)S(1)}, u32[]{:S(2)}, u32[]{:S(2)}) collective-permute-start(bf16[40,16,256]{2,1,0:T(8,128)(2,1)S(1)} %pad_maximum_fusion.2.rest_8_.rest_0_), channel_id=1, source_target_pairs={{0,8},{1,9},{2,10},{3,11},{4,12},{5,13},{6,14},{7,15},{8,0},{9,1},... | collective-permute-start | bytes 983048 | tf_op jit(solution)/shard_map/ppermute | solution.py:27
  32.8 1.5 collective-permute-start.14
  34.4 14.0 %collective-permute-done.16.rest_11_.rest_3_ = bf16[40,16,256]{2,1,0:T(8,128)(2,1)S(1)} collective-permute-done((bf16[40,16,256]{2,1,0:T(8,128)(2,1)S(1)}, bf16[40,16,256]{2,1,0:T(8,128)(2,1)S(1)}, u32[]{:S(2)}, u32[]{:S(2)}) %collective-permute-start.16) | collective-permute-done | bytes 327712 | tf_op jit(solution)/shard_map/ppermute | solution.py:27
  51.9 23.5 %shard_map.73 = (bf16[4,2,16,16,256]{4,3,2,1,0:T(8,128)(2,1)}, f32[4,2,16,16,256]{4,3,2,1,0:T(8,128)}) custom-call(s32[4]{0:T(128)} %ms_ref.7, s32[128]{0:T(128)} %li_ref.7, s32[2]{0:T(128)} %pad_add_fusion.ids_ref, f32[4,5]{1,0:T(4,128)} %w_ref.7, bf16[4,2,16,256,256]{4,3,2,1,0:T(8,128)(2,1)} %q_ref.3, bf16[4,2,16,256,256]{4,3,2,1,0:T(8,128)(2,1)} %q_ref.3, ...), custom_call_target="tpu_custom_call" | custom-call | tf_op jit(solution)/shard_map/pallas_call | solution.py:115
  76.9 6.8 %shard_map.75 = (bf16[4,2,6,16,256]{4,3,2,1,0:T(8,128)(2,1)}, f32[4,2,6,16,256]{4,3,2,1,0:T(8,128)}) custom-call(s32[4]{0:T(128)} %ms_ref.7, s32[128]{0:T(128)} %li_ref.7, s32[2]{0:T(128)} %pad_add_fusion.ids_ref, f32[4,5]{1,0:T(4,128)} %w_ref.7, bf16[4,2,256,256]{3,2,1,0:T(8,128)(2,1)} %collective-permute-done.9.above_ref, ...), custom_call_target="tpu_custom_call" | custom-call | tf_op jit(solution)/shard_map/pallas_call | solution.py:217
  84.4 6.7 %shard_map.74 = (bf16[4,2,6,16,256]{4,3,2,1,0:T(8,128)(2,1)}, f32[4,2,6,16,256]{4,3,2,1,0:T(8,128)}) custom-call(s32[4]{0:T(128)} %ms_ref.7, s32[128]{0:T(128)} %li_ref.7, s32[2]{0:T(128)} %pad_add_fusion.ids_ref, f32[4,5]{1,0:T(4,128)} %w_ref.7, bf16[4,2,256,256]{3,2,1,0:T(8,128)(2,1)} %collective-permute-done.9.above_ref, ...), custom_call_target="tpu_custom_call" | custom-call | tf_op jit(solution)/shard_map/pallas_call | solution.py:217
  91.2 23.7 %shard_map.76 = (bf16[4,2,16,16,256]{4,3,2,1,0:T(8,128)(2,1)}, f32[4,2,16,16,256]{4,3,2,1,0:T(8,128)}) custom-call(s32[4]{0:T(128)} %ms_ref.7, s32[128]{0:T(128)} %li_ref.7, s32[2]{0:T(128)} %pad_add_fusion.ids_ref, f32[4,5]{1,0:T(4,128)} %w_ref.7, bf16[4,2,16,256,256]{4,3,2,1,0:T(8,128)(2,1)} %q_ref.3, bf16[4,2,16,256,256]{4,3,2,1,0:T(8,128)(2,1)} %q_ref.3, ...), custom_call_target="tpu_custom_call" | custom-call | tf_op jit(solution)/shard_map/pallas_call | solution.py:115
  117.2 1.6 convert_add_fusion.1
  119.8 3.6 %collective-permute-start.25 = (bf16[2,20,16,256]{3,2,1,0:T(8,128)(2,1)S(1)}, bf16[2,20,16,256]{3,2,1,0:T(8,128)(2,1)S(1)}, u32[]{:S(2)}, u32[]{:S(2)}) collective-permute-start(bf16[2,20,16,256]{3,2,1,0:T(8,128)(2,1)S(1)} %get-tuple-element.26), channel_id=1, source_target_pairs={{0,8},{1,9},{2,10},{3,11},{4,12},{5,13},{6,14},{7,15},{8,0},{9,1},... | collective-permute-start | bytes 983048 | tf_op jit(solution)/shard_map/ppermute | solution.py:27
  125.2 2.1 %collective-permute-start.30 = (bf16[2,16,16,256]{3,2,1,0:T(8,128)(2,1)S(1)}, bf16[2,16,16,256]{3,2,1,0:T(8,128)(2,1)S(1)}, u32[]{:S(2)}, u32[]{:S(2)}) collective-permute-start(bf16[2,16,16,256]{3,2,1,0:T(8,128)(2,1)S(1)} %get-tuple-element.28), channel_id=1, source_target_pairs={{0,4},{1,5},{2,6},{3,7},{4,8},{5,9},{6,10},{7,11},{8,12},{9,13},{1... | collective-permute-start | bytes 786440 | tf_op jit(solution)/shard_map/ppermute | solution.py:27
  127.8 4.2 %collective-permute-done.23 = bf16[2,20,16,256]{3,2,1,0:T(8,128)(2,1)S(1)} collective-permute-done((bf16[2,20,16,256]{3,2,1,0:T(8,128)(2,1)S(1)}, bf16[2,20,16,256]{3,2,1,0:T(8,128)(2,1)S(1)}, u32[]{:S(2)}, u32[]{:S(2)}) %collective-permute-start.23) | collective-permute-done | bytes 327712 | tf_op jit(solution)/shard_map/ppermute | solution.py:27
  132.5 6.5 %collective-permute-done.25 = bf16[2,20,16,256]{3,2,1,0:T(8,128)(2,1)S(1)} collective-permute-done((bf16[2,20,16,256]{3,2,1,0:T(8,128)(2,1)S(1)}, bf16[2,20,16,256]{3,2,1,0:T(8,128)(2,1)S(1)}, u32[]{:S(2)}, u32[]{:S(2)}) %collective-permute-start.25) | collective-permute-done | bytes 327712 | tf_op jit(solution)/shard_map/ppermute | solution.py:27
  139.4 2.9 %collective-permute-start.26 = (bf16[20,16,256]{2,1,0:T(8,128)(2,1)S(1)}, bf16[20,16,256]{2,1,0:T(8,128)(2,1)S(1)}, u32[]{:S(2)}, u32[]{:S(2)}) collective-permute-start(bf16[20,16,256]{2,1,0:T(8,128)(2,1)S(1)} %fusion.10), channel_id=1, source_target_pairs={{0,2},{1,3},{2,0},{3,1},{4,6},{5,7},{6,4},{7,5},{8,10},{9,11},{10,... | collective-permute-start | bytes 491528 | tf_op jit(solution)/shard_map/ppermute | solution.py:27
  143.3 6.3 %collective-permute-done.32 = bf16[2,16,16,256]{3,2,1,0:T(8,128)(2,1)S(1)} collective-permute-done((bf16[2,16,16,256]{3,2,1,0:T(8,128)(2,1)S(1)}, bf16[2,16,16,256]{3,2,1,0:T(8,128)(2,1)S(1)}, u32[]{:S(2)}, u32[]{:S(2)}) %collective-permute-start.32) | collective-permute-done | bytes 262176 | tf_op jit(solution)/shard_map/ppermute | solution.py:27
  149.7 2.9 %collective-permute-start.33 = (bf16[16,16,256]{2,1,0:T(8,128)(2,1)S(1)}, bf16[16,16,256]{2,1,0:T(8,128)(2,1)S(1)}, u32[]{:S(2)}, u32[]{:S(2)}) collective-permute-start(bf16[16,16,256]{2,1,0:T(8,128)(2,1)S(1)} %fusion.11), channel_id=1, source_target_pairs={{0,2},{1,3},{2,0},{3,1},{4,6},{5,7},{6,4},{7,5},{8,10},{9,11},{10,... | collective-permute-start | bytes 393224 | tf_op jit(solution)/shard_map/ppermute | solution.py:27
  152.7 4.4 %collective-permute-start.27 = (f32[2,16,256]{2,1,0:T(8,128)S(1)}, f32[2,16,256]{2,1,0:T(8,128)S(1)}, u32[]{:S(2)}, u32[]{:S(2)}) collective-permute-start(f32[2,16,256]{2,1,0:T(8,128)S(1)} %get-tuple-element.41), channel_id=1, source_target_pairs={{0,16},{16,32},{32,48},{48,64},{64,80},{80,96},{96,112},{1,17},{17... | collective-permute-start | bytes 98312 | tf_op jit(solution)/shard_map/ppermute | solution.py:31
  158.7 5.9 %collective-permute-done.28 = f32[2,16,256]{2,1,0:T(8,128)S(1)} collective-permute-done((f32[2,16,256]{2,1,0:T(8,128)S(1)}, f32[2,16,256]{2,1,0:T(8,128)S(1)}, u32[]{:S(2)}, u32[]{:S(2)}) %collective-permute-start.28) | collective-permute-done | bytes 32800 | tf_op jit(solution)/shard_map/ppermute | solution.py:31
  (130 shorter events, 22.8 us)
Async XLA Ops:
  10.0 9.1 %collective-permute-start.13 = (bf16[20,16,256]{2,1,0:T(8,128)(2,1)S(1)}, bf16[20,16,256]{2,1,0:T(8,128)(2,1)S(1)}, u32[]{:S(2)}, u32[]{:S(2)}) collective-permute-start(bf16[20,16,256]{2,1,0:T(8,128)(2,1)S(1)} %pad_maximum_fusion.4), channel_id=1, source_target_pairs={{0,2},{1,3},{2,0},{3,1},{4,6},{5,7},{6,4},{7,5},{8,10},{9,11},{10,... | collective-permute-start | bytes 491528 | tf_op jit(solution)/shard_map/ppermute | solution.py:27
  13.3 9.0 %collective-permute-start.4 = (bf16[32,16,256]{2,1,0:T(8,128)(2,1)S(1)}, bf16[32,16,256]{2,1,0:T(8,128)(2,1)S(1)}, u32[]{:S(2)}, u32[]{:S(2)}) collective-permute-start(bf16[32,16,256]{2,1,0:T(8,128)(2,1)S(1)} %pad_maximum_fusion.3.rest_0_), channel_id=1, source_target_pairs={{0,1},{1,0},{2,3},{3,2},{4,5},{5,4},{6,7},{7,6},{8,9},{9,8},{10,11... | collective-permute-start | bytes 786440 | tf_op jit(solution)/shard_map/ppermute | solution.py:27
  13.4 10.3 %collective-permute-start.3 = (bf16[32,16,256]{2,1,0:T(8,128)(2,1)S(1)}, bf16[32,16,256]{2,1,0:T(8,128)(2,1)S(1)}, u32[]{:S(2)}, u32[]{:S(2)}) collective-permute-start(bf16[32,16,256]{2,1,0:T(8,128)(2,1)S(1)} %pad_maximum_fusion.3.rest_0_), channel_id=1, source_target_pairs={{0,4},{1,5},{2,6},{3,7},{4,8},{5,9},{6,10},{7,11},{8,12},{9,13},{1... | collective-permute-start | bytes 786440 | tf_op jit(solution)/shard_map/ppermute | solution.py:27
  14.9 15.3 %collective-permute-start.2 = (bf16[32,16,256]{2,1,0:T(8,128)(2,1)S(1)}, bf16[32,16,256]{2,1,0:T(8,128)(2,1)S(1)}, u32[]{:S(2)}, u32[]{:S(2)}) collective-permute-start(bf16[32,16,256]{2,1,0:T(8,128)(2,1)S(1)} %pad_maximum_fusion.3.rest_0_), channel_id=1, source_target_pairs={{0,8},{1,9},{2,10},{3,11},{4,12},{5,13},{6,14},{7,15},{8,0},{9,1},... | collective-permute-start | bytes 786440 | tf_op jit(solution)/shard_map/ppermute | solution.py:27
  17.7 13.2 %collective-permute-start.1 = (bf16[32,16,256]{2,1,0:T(8,128)(2,1)S(1)}, bf16[32,16,256]{2,1,0:T(8,128)(2,1)S(1)}, u32[]{:S(2)}, u32[]{:S(2)}) collective-permute-start(bf16[32,16,256]{2,1,0:T(8,128)(2,1)S(1)} %pad_maximum_fusion.3.rest_0_), channel_id=1, source_target_pairs={{0,12},{1,13},{2,14},{3,15},{4,0},{5,1},{6,2},{7,3},{8,4},{9,5},{1... | collective-permute-start | bytes 786440 | tf_op jit(solution)/shard_map/ppermute | solution.py:27
  19.2 13.7 %collective-permute-start.17 = (bf16[40,16,256]{2,1,0:T(8,128)(2,1)S(1)}, bf16[40,16,256]{2,1,0:T(8,128)(2,1)S(1)}, u32[]{:S(2)}, u32[]{:S(2)}) collective-permute-start(bf16[40,16,256]{2,1,0:T(8,128)(2,1)S(1)} %pad_maximum_fusion.2.rest_8_.rest_0_), channel_id=1, source_target_pairs={{0,1},{1,0},{2,3},{3,2},{4,5},{5,4},{6,7},{7,6},{8,9},{9,8},{10,11... | collective-permute-start | bytes 983048 | tf_op jit(solution)/shard_map/ppermute | solution.py:27
  22.3 53.3 %collective-permute-start.10 = (bf16[4,2,256,256]{3,2,1,0:T(8,128)(2,1)}, bf16[4,2,256,256]{3,2,1,0:T(8,128)(2,1)S(1)}, u32[]{:S(2)}, u32[]{:S(2)}) collective-permute-start(bf16[4,2,256,256]{3,2,1,0:T(8,128)(2,1)} %get-tuple-element.21), channel_id=1, source_target_pairs={{16,0},{32,16},{48,32},{64,48},{80,64},{96,80},{112,96},{17,1},{33... | collective-permute-start | bytes 3145736 | tf_op jit(solution)/shard_map/ppermute | solution.py:31
  23.7 52.0 %collective-permute-start.9 = (bf16[4,2,256,256]{3,2,1,0:T(8,128)(2,1)}, bf16[4,2,256,256]{3,2,1,0:T(8,128)(2,1)}, u32[]{:S(2)}, u32[]{:S(2)}) collective-permute-start(bf16[4,2,256,256]{3,2,1,0:T(8,128)(2,1)} %get-tuple-element.22), channel_id=1, source_target_pairs={{0,16},{16,32},{32,48},{48,64},{64,80},{80,96},{96,112},{1,17},{17... | collective-permute-start | bytes 3145736 | tf_op jit(solution)/shard_map/ppermute | solution.py:31
  30.3 18.0 %collective-permute-start.16 = (bf16[40,16,256]{2,1,0:T(8,128)(2,1)S(1)}, bf16[40,16,256]{2,1,0:T(8,128)(2,1)S(1)}, u32[]{:S(2)}, u32[]{:S(2)}) collective-permute-start(bf16[40,16,256]{2,1,0:T(8,128)(2,1)S(1)} %pad_maximum_fusion.2.rest_8_.rest_0_), channel_id=1, source_target_pairs={{0,4},{1,5},{2,6},{3,7},{4,8},{5,9},{6,10},{7,11},{8,12},{9,13},{1... | collective-permute-start | bytes 983048 | tf_op jit(solution)/shard_map/ppermute | solution.py:27
  30.9 17.4 %collective-permute-start.15 = (bf16[40,16,256]{2,1,0:T(8,128)(2,1)S(1)}, bf16[40,16,256]{2,1,0:T(8,128)(2,1)S(1)}, u32[]{:S(2)}, u32[]{:S(2)}) collective-permute-start(bf16[40,16,256]{2,1,0:T(8,128)(2,1)S(1)} %pad_maximum_fusion.2.rest_8_.rest_0_), channel_id=1, source_target_pairs={{0,8},{1,9},{2,10},{3,11},{4,12},{5,13},{6,14},{7,15},{8,0},{9,1},... | collective-permute-start | bytes 983048 | tf_op jit(solution)/shard_map/ppermute | solution.py:27
  32.8 16.1 %collective-permute-start.14 = (bf16[40,16,256]{2,1,0:T(8,128)(2,1)S(1)}, bf16[40,16,256]{2,1,0:T(8,128)(2,1)S(1)}, u32[]{:S(2)}, u32[]{:S(2)}) collective-permute-start(bf16[40,16,256]{2,1,0:T(8,128)(2,1)S(1)} %pad_maximum_fusion.2.rest_8_.rest_0_), channel_id=1, source_target_pairs={{0,12},{1,13},{2,14},{3,15},{4,0},{5,1},{6,2},{7,3},{8,4},{9,5},{1... | collective-permute-start | bytes 983048 | tf_op jit(solution)/shard_map/ppermute | solution.py:27
  49.9 25.6 %collective-permute-start.20 = (bf16[40,16,256]{2,1,0:T(8,128)(2,1)S(1)}, bf16[40,16,256]{2,1,0:T(8,128)(2,1)S(1)}, u32[]{:S(2)}, u32[]{:S(2)}) collective-permute-start(bf16[40,16,256]{2,1,0:T(8,128)(2,1)S(1)} %collective-permute-done.16.rest_11_.rest_3_), channel_id=1, source_target_pairs={{0,1},{1,0},{2,3},{3,2},{4,5},{5,4},{6,7},{7,6},{8,9},{9,8},{10,11... | collective-permute-start | bytes 983048 | tf_op jit(solution)/shard_map/ppermute | solution.py:27
  50.2 25.4 %collective-permute-start.19 = (bf16[40,16,256]{2,1,0:T(8,128)(2,1)S(1)}, bf16[40,16,256]{2,1,0:T(8,128)(2,1)S(1)}, u32[]{:S(2)}, u32[]{:S(2)}) collective-permute-start(bf16[40,16,256]{2,1,0:T(8,128)(2,1)S(1)} %collective-permute-done.15.rest_10_.rest_2_), channel_id=1, source_target_pairs={{0,1},{1,0},{2,3},{3,2},{4,5},{5,4},{6,7},{7,6},{8,9},{9,8},{10,11... | collective-permute-start | bytes 983048 | tf_op jit(solution)/shard_map/ppermute | solution.py:27
  50.6 25.1 %collective-permute-start.18 = (bf16[40,16,256]{2,1,0:T(8,128)(2,1)S(1)}, bf16[40,16,256]{2,1,0:T(8,128)(2,1)S(1)}, u32[]{:S(2)}, u32[]{:S(2)}) collective-permute-start(bf16[40,16,256]{2,1,0:T(8,128)(2,1)S(1)} %collective-permute-done.14.rest_9_.rest_1_), channel_id=1, source_target_pairs={{0,1},{1,0},{2,3},{3,2},{4,5},{5,4},{6,7},{7,6},{8,9},{9,8},{10,11... | collective-permute-start | bytes 983048 | tf_op jit(solution)/shard_map/ppermute | solution.py:27
  75.5 40.7 %collective-permute-start.8 = (bf16[4,2,16,16,256]{4,3,2,1,0:T(8,128)(2,1)}, bf16[4,2,16,16,256]{4,3,2,1,0:T(8,128)(2,1)}, u32[]{:S(2)}, u32[]{:S(2)}) collective-permute-start(bf16[4,2,16,16,256]{4,3,2,1,0:T(8,128)(2,1)} %get-tuple-element.14), channel_id=1, source_target_pairs={{0,1},{1,0},{2,3},{3,2},{4,5},{5,4},{6,7},{7,6},{8,9},{9,8},{10,11... | collective-permute-start | bytes 3145736 | tf_op jit(solution)/shard_map/ppermute | solution.py:27
  83.6 31.6 %collective-permute-start.22 = (bf16[4,2,6,16,256]{4,3,2,1,0:T(8,128)(2,1)}, bf16[4,2,6,16,256]{4,3,2,1,0:T(8,128)(2,1)S(1)}, u32[]{:S(2)}, u32[]{:S(2)}) collective-permute-start(bf16[4,2,6,16,256]{4,3,2,1,0:T(8,128)(2,1)} %get-tuple-element.18), channel_id=1, source_target_pairs={{0,1},{1,0},{2,3},{3,2},{4,5},{5,4},{6,7},{7,6},{8,9},{9,8},{10,11... | collective-permute-start | bytes 1179656 | tf_op jit(solution)/shard_map/ppermute | solution.py:27
  91.1 24.3 %collective-permute-start.21 = (bf16[4,2,6,16,256]{4,3,2,1,0:T(8,128)(2,1)}, bf16[4,2,6,16,256]{4,3,2,1,0:T(8,128)(2,1)S(1)}, u32[]{:S(2)}, u32[]{:S(2)}) collective-permute-start(bf16[4,2,6,16,256]{4,3,2,1,0:T(8,128)(2,1)} %get-tuple-element.16), channel_id=1, source_target_pairs={{0,1},{1,0},{2,3},{3,2},{4,5},{5,4},{6,7},{7,6},{8,9},{9,8},{10,11... | collective-permute-start | bytes 1179656 | tf_op jit(solution)/shard_map/ppermute | solution.py:27
  119.4 12.6 %collective-permute-start.23 = (bf16[2,20,16,256]{3,2,1,0:T(8,128)(2,1)S(1)}, bf16[2,20,16,256]{3,2,1,0:T(8,128)(2,1)S(1)}, u32[]{:S(2)}, u32[]{:S(2)}) collective-permute-start(bf16[2,20,16,256]{3,2,1,0:T(8,128)(2,1)S(1)} %get-tuple-element.25), channel_id=1, source_target_pairs={{0,4},{1,5},{2,6},{3,7},{4,8},{5,9},{6,10},{7,11},{8,12},{9,13},{1... | collective-permute-start | bytes 983048 | tf_op jit(solution)/shard_map/ppermute | solution.py:27
  119.8 19.2 %collective-permute-start.25 = (bf16[2,20,16,256]{3,2,1,0:T(8,128)(2,1)S(1)}, bf16[2,20,16,256]{3,2,1,0:T(8,128)(2,1)S(1)}, u32[]{:S(2)}, u32[]{:S(2)}) collective-permute-start(bf16[2,20,16,256]{3,2,1,0:T(8,128)(2,1)S(1)} %get-tuple-element.26), channel_id=1, source_target_pairs={{0,8},{1,9},{2,10},{3,11},{4,12},{5,13},{6,14},{7,15},{8,0},{9,1},... | collective-permute-start | bytes 983048 | tf_op jit(solution)/shard_map/ppermute | solution.py:27
  123.4 15.8 %collective-permute-start.24 = (bf16[2,20,16,256]{3,2,1,0:T(8,128)(2,1)S(1)}, bf16[2,20,16,256]{3,2,1,0:T(8,128)(2,1)S(1)}, u32[]{:S(2)}, u32[]{:S(2)}) collective-permute-start(bf16[2,20,16,256]{3,2,1,0:T(8,128)(2,1)S(1)} %get-tuple-element.27), channel_id=1, source_target_pairs={{0,12},{1,13},{2,14},{3,15},{4,0},{5,1},{6,2},{7,3},{8,4},{9,5},{1... | collective-permute-start | bytes 983048 | tf_op jit(solution)/shard_map/ppermute | solution.py:27
  125.2 18.1 %collective-permute-start.30 = (bf16[2,16,16,256]{3,2,1,0:T(8,128)(2,1)S(1)}, bf16[2,16,16,256]{3,2,1,0:T(8,128)(2,1)S(1)}, u32[]{:S(2)}, u32[]{:S(2)}) collective-permute-start(bf16[2,16,16,256]{3,2,1,0:T(8,128)(2,1)S(1)} %get-tuple-element.28), channel_id=1, source_target_pairs={{0,4},{1,5},{2,6},{3,7},{4,8},{5,9},{6,10},{7,11},{8,12},{9,13},{1... | collective-permute-start | bytes 786440 | tf_op jit(solution)/shard_map/ppermute | solution.py:27
  127.3 22.3 %collective-permute-start.32 = (bf16[2,16,16,256]{3,2,1,0:T(8,128)(2,1)S(1)}, bf16[2,16,16,256]{3,2,1,0:T(8,128)(2,1)S(1)}, u32[]{:S(2)}, u32[]{:S(2)}) collective-permute-start(bf16[2,16,16,256]{3,2,1,0:T(8,128)(2,1)S(1)} %get-tuple-element.29), channel_id=1, source_target_pairs={{0,8},{1,9},{2,10},{3,11},{4,12},{5,13},{6,14},{7,15},{8,0},{9,1},... | collective-permute-start | bytes 786440 | tf_op jit(solution)/shard_map/ppermute | solution.py:27
  132.0 17.5 %collective-permute-start.31 = (bf16[2,16,16,256]{3,2,1,0:T(8,128)(2,1)S(1)}, bf16[2,16,16,256]{3,2,1,0:T(8,128)(2,1)S(1)}, u32[]{:S(2)}, u32[]{:S(2)}) collective-permute-start(bf16[2,16,16,256]{3,2,1,0:T(8,128)(2,1)S(1)} %get-tuple-element.30), channel_id=1, source_target_pairs={{0,12},{1,13},{2,14},{3,15},{4,0},{5,1},{6,2},{7,3},{8,4},{9,5},{1... | collective-permute-start | bytes 786440 | tf_op jit(solution)/shard_map/ppermute | solution.py:27
  139.4 13.2 %collective-permute-start.26 = (bf16[20,16,256]{2,1,0:T(8,128)(2,1)S(1)}, bf16[20,16,256]{2,1,0:T(8,128)(2,1)S(1)}, u32[]{:S(2)}, u32[]{:S(2)}) collective-permute-start(bf16[20,16,256]{2,1,0:T(8,128)(2,1)S(1)} %fusion.10), channel_id=1, source_target_pairs={{0,2},{1,3},{2,0},{3,1},{4,6},{5,7},{6,4},{7,5},{8,10},{9,11},{10,... | collective-permute-start | bytes 491528 | tf_op jit(solution)/shard_map/ppermute | solution.py:27
  (33 other events, 318.5 us)

commit v3 on v2

--- a/solution.py
+++ b/solution.py
@@ -52,85 +52,103 @@
     ms_ref, li_ref, ids_ref, w_ref, p_ref, q_ref, ky_ref, kx_ref, *rest, levels, inv
 ):
     pieces = rest[:8]
-    send_ref, keep_ref, gs, acc, *rings = rest[8:]
-    t = pl.program_id(0)
+    send_ref, keep_ref, gs, acc, fresh, *rings = rest[8:]
+    u = pl.program_id(0)
     mem = ids_ref[0]
     base = ids_ref[1] * levels
 
-    @pl.when(t == 0)
+    @pl.when(u == 0)
     def _():
         for ring in rings:
-            for slot in (3, 4):
-                ring[slot] = jnp.zeros(ring.shape[1:], F32)
-
-    lo = t - 2
-    level = jnp.minimum(t, levels - 1)
-    newest = lax.rem(t, 5)
-    slots = [lax.rem(t + 1 + d, 5) for d in range(5)]
-
-    def coef(k, d):
+            ring[4] = jnp.zeros(ring.shape[1:], F32)
+            ring[5] = jnp.zeros(ring.shape[1:], F32)
+        fresh[...] = jnp.zeros(fresh.shape, F32)
+
+    pair = 2 * jnp.minimum(u, levels // 2 - 1)
+    slots = [lax.rem(2 * u + d, 6) for d in range(6)]
+
+    def coef(k, lo, d):
         other = lo + d
         a = jnp.clip(base + lo, 0, 127)
         b = jnp.clip(base + other, 0, 127)
         ok = (other >= 0) & (other < levels) & (li_ref[a] == li_ref[b])
         return jnp.where(ok, w_ref[ms_ref[k], d + 2], 0.0) * inv
 
-    for cr in range(2):
-        for hr in range(2):
-            for j in range(4):
-                block = pieces[cr * 4 + j][hr * levels + level]
-                gs[pl.ds(rows_at(mem, j, hr, cr), 16), :] = block
-    g = gs[...]
-
-    for k in range(4):
-        s = ms_ref[k]
-        rings[k][newest] = field(p_ref[k, 0, 0], g, ky_ref[s], kx_ref[s]).astype(F32)
-        cs = [coef(k, d) for d in range(-2, 3)]
+    for i in range(2):
         for cr in range(2):
             for hr in range(2):
                 for j in range(4):
-                    place = cr * 8 + hr * 4 + j
-                    r0 = rows_at(mem, j, hr, cr)
-                    mix = None
-                    for d in range(5):
-                        term = cs[d] * rings[k][slots[d], pl.ds(r0, 16), :]
-                        mix = term if mix is None else mix + term
-                    mix = mix * q_ref[k, 0, 0, pl.ds(r0, 16), :].astype(F32)
-                    if k:
-                        mix = mix + acc[place]
-                    if k < 3:
-                        acc[place] = mix
-                    elif cr:
-                        send_ref[j, hr, 0] = mix.astype(BF)
-                    else:
-                        keep_ref[j, hr, 0] = mix
+                    block = pieces[cr * 4 + j][hr * levels + pair + i]
+                    gs[i, pl.ds(rows_at(mem, j, hr, cr), 16), :] = block
+
+    for k in range(4):
+        for i in range(2):
+            rings[k][slots[4 + i]] = fresh[i, k]
+
+    gate = None
+    for i in range(2):
+        g = gs[i]
+        for k in range(4):
+            s = ms_ref[k]
+            rows = jnp.dot(ky_ref[s], p_ref[k, 0, i] * g, preferred_element_type=F32)
+            gate = rows if gate is None else gate
+            fresh[i, k] = lax.dot_general(
+                rows.astype(BF), kx_ref[s], (((1,), (1,)), ((), ())), preferred_element_type=F32
+            )
+
+    for i in range(2):
+        for k in range(4):
+            if i == 0:
+                rings[k][6, 0:8, 0:128] = gate[0:8, 0:128]
+            cs = [coef(k, 2 * u - 4 + i, d) for d in range(-2, 3)]
+            for cr in range(2):
+                for hr in range(2):
+                    for j in range(4):
+                        place = cr * 8 + hr * 4 + j
+                        r0 = rows_at(mem, j, hr, cr)
+                        mix = None
+                        for d in range(5):
+                            term = cs[d] * rings[k][slots[i + d], pl.ds(r0, 16), :]
+                            mix = term if mix is None else mix + term
+                        mix = mix * q_ref[k, 0, i, pl.ds(r0, 16), :].astype(F32)
+                        if k:
+                            mix = mix + acc[i, place]
+                        if k < 3:
+                            acc[i, place] = mix
+                        elif cr:
+                            send_ref[j, hr, i] = mix.astype(BF)
+                        else:
+                            keep_ref[j, hr, i] = mix
 
 
 def own_part(v, ms, li, ids, w, p, ky, kx, pieces, inv):
     levels = p.shape[2]
     smem = pl.BlockSpec(memory_space=pltpu.SMEM)
-    whole = pl.BlockSpec((4, 256, 256), lambda t, *_: (0, 0, 0))
-    pblock = (4, 1, 1, 256, 256)
-    part = pl.BlockSpec((4, 2, 1, 16, 256), lambda t, *_: (0, 0, jnp.maximum(t - 2, 0), 0, 0))
+    whole = pl.BlockSpec((4, 256, 256), lambda u, *_: (0, 0, 0))
+    pblock = (4, 1, 2, 256, 256)
+    part = pl.BlockSpec((4, 2, 2, 16, 256), lambda u, *_: (0, 0, jnp.maximum(u - 2, 0), 0, 0))
     return pl.pallas_call(
         functools.partial(own_kernel, levels=levels, inv=inv),
         grid_spec=pltpu.PrefetchScalarGridSpec(
             num_scalar_prefetch=3,
-            grid=(levels + 2,),
+            grid=(levels // 2 + 2,),
             in_specs=[
                 smem,
-                pl.BlockSpec(pblock, lambda t, *_: (0, v, jnp.minimum(t, levels - 1), 0, 0)),
-                pl.BlockSpec(pblock, lambda t, *_: (0, v, jnp.maximum(t - 2, 0), 0, 0)),
+                pl.BlockSpec(
+                    pblock, lambda u, *_: (0, v, jnp.minimum(u, levels // 2 - 1), 0, 0)
+                ),
+                pl.BlockSpec(pblock, lambda u, *_: (0, v, jnp.maximum(u - 2, 0), 0, 0)),
                 whole,
                 whole,
             ]
-            + [pl.BlockSpec((2 * levels, 16, 256), lambda t, *_: (0, 0, 0))] * 8,
+            + [pl.BlockSpec((2 * levels, 16, 256), lambda u, *_: (0, 0, 0))] * 8,
             out_specs=[part, part],
             scratch_shapes=[
-                pltpu.VMEM((256, 256), BF),
-                pltpu.VMEM((16, 16, 256), F32),
+                pltpu.VMEM((2, 256, 256), BF),
+                pltpu.VMEM((2, 16, 16, 256), F32),
+                pltpu.VMEM((2, 4, 256, 256), F32),
             ]
-            + [pltpu.VMEM((5, 256, 256), F32)] * 4,
+            + [pltpu.VMEM((7, 256, 256), F32)] * 4,
         ),
         out_shape=[
             jax.ShapeDtypeStruct((4, 2, levels, 16, 256), BF),

time: 168 us -> 159 us (0.946)
  Pallas kernels: 60.7 us -> 52.1 us
    pallas_call x2, Pallas kernels: 47.2 us -> 38.6 us  [own_part(): pl.pallas_call(functools.partial(own_kernel, levels=levels, inv=inv), gri...]
  transfers between devices with their start and end apart: 34 -> 34, of which waited for: 14 -> 14; matrix products, arithmetic and copies ran while one was open for 5% -> 5% of each run, Pallas kernels for 37% -> 33%
where the time goes in v3:
time: 159 us; the launch traced here: 157 us
  Pallas kernels  52.1 us (33%)
  starting transfers between devices  49.7 us (31%)
  waiting for transfers between devices  40.2 us (25%)
  local copies, waits for them, and re-layouts  9.58 us (6%)
  other arithmetic  4.88 us (3%)
    pallas_call x2, Pallas kernels, own_part(): pl.pallas_call(functools.partial(own_kernel, levels=levels, inv=inv), gri...  38.6 us
    ppermute x28, waiting for transfers between devices, move(): return lax.ppermute(value, 'mem', pairs_of(dx, dh, dc))  33.8 us
    ppermute x28, starting transfers between devices, move(): return lax.ppermute(value, 'mem', pairs_of(dx, dh, dc))  31.3 us
    ppermute x6, starting transfers between devices, shift(): return lax.ppermute(value, 'lev', pairs)  18.5 us
    pallas_call x2, Pallas kernels, edge_part(): pl.pallas_call(functools.partial(edge_kernel, v=v, levels=levels, inv=inv...  13.5 us
    ppermute x6, waiting for transfers between devices, shift(): return lax.ppermute(value, 'lev', pairs)  6.48 us
    unnamed x46, local copies, waits for them, and re-layouts  3.53 us
  transfers between devices with their start and end apart: 34, of which 14 were waited for; matrix products, arithmetic and copies ran while one was open for 5% of the time, Pallas kernels for 33%

profile of v3, /device:TPU:0, one launch (start us, length us, event | category | flops | bytes accessed | tf_op | source)
XLA Modules:
  0.0 157.1 jit_solution(705115646602504341)
XLA Ops:
  0.7 3.6 %collective-permute-start.11 = (bf16[2,16,256]{2,1,0:T(8,128)(2,1)S(1)}, bf16[2,16,256]{2,1,0:T(8,128)(2,1)S(1)}, u32[]{:S(2)}, u32[]{:S(2)}) collective-permute-start(bf16[2,16,256]{2,1,0:T(8,128)(2,1)S(1)} %get-tuple-element.37), channel_id=1, source_target_pairs={{0,16},{16,32},{32,48},{48,64},{64,80},{80,96},{96,112},{1,17},{17... | collective-permute-start | bytes 49160 | tf_op jit(solution)/shard_map/ppermute | solution.py:31
  6.6 3.0 %collective-permute-start = (bf16[16,16,256]{2,1,0:T(8,128)(2,1)S(1)}, bf16[16,16,256]{2,1,0:T(8,128)(2,1)S(1)}, u32[]{:S(2)}, u32[]{:S(2)}) collective-permute-start(bf16[16,16,256]{2,1,0:T(8,128)(2,1)S(1)} %get-tuple-element.36), channel_id=1, source_target_pairs={{0,2},{1,3},{2,0},{3,1},{4,6},{5,7},{6,4},{7,5},{8,10},{9,11},{10,... | collective-permute-start | bytes 393224 | tf_op jit(solution)/shard_map/ppermute | solution.py:27
  10.0 3.1 %collective-permute-start.13 = (bf16[20,16,256]{2,1,0:T(8,128)(2,1)S(1)}, bf16[20,16,256]{2,1,0:T(8,128)(2,1)S(1)}, u32[]{:S(2)}, u32[]{:S(2)}) collective-permute-start(bf16[20,16,256]{2,1,0:T(8,128)(2,1)S(1)} %pad_maximum_fusion.4), channel_id=1, source_target_pairs={{0,2},{1,3},{2,0},{3,1},{4,6},{5,7},{6,4},{7,5},{8,10},{9,11},{10,... | collective-permute-start | bytes 491528 | tf_op jit(solution)/shard_map/ppermute | solution.py:27
  13.4 1.6 collective-permute-start.3
  14.9 2.7 %collective-permute-start.2 = (bf16[32,16,256]{2,1,0:T(8,128)(2,1)S(1)}, bf16[32,16,256]{2,1,0:T(8,128)(2,1)S(1)}, u32[]{:S(2)}, u32[]{:S(2)}) collective-permute-start(bf16[32,16,256]{2,1,0:T(8,128)(2,1)S(1)} %pad_maximum_fusion.3.rest_0_), channel_id=1, source_target_pairs={{0,8},{1,9},{2,10},{3,11},{4,12},{5,13},{6,14},{7,15},{8,0},{9,1},... | collective-permute-start | bytes 786440 | tf_op jit(solution)/shard_map/ppermute | solution.py:27
  19.3 3.0 %slice_bitcast_fusion = (bf16[4,2,256,256]{3,2,1,0:T(8,128)(2,1)}, bf16[4,2,256,256]{3,2,1,0:T(8,128)(2,1)}) fusion(bf16[4,2,16,256,256]{4,3,2,1,0:T(8,128)(2,1)} %q_ref.3), kind=kLoop, calls=%fused_computation.4 | loop fusion | bytes 4194304 | tf_op jit(solution)/shard_map/squeeze | solution.py:296
  23.7 6.6 %collective-permute-start.9 = (bf16[4,2,256,256]{3,2,1,0:T(8,128)(2,1)}, bf16[4,2,256,256]{3,2,1,0:T(8,128)(2,1)}, u32[]{:S(2)}, u32[]{:S(2)}) collective-permute-start(bf16[4,2,256,256]{3,2,1,0:T(8,128)(2,1)} %get-tuple-element.22), channel_id=1, source_target_pairs={{0,16},{16,32},{32,48},{48,64},{64,80},{80,96},{96,112},{1,17},{17... | collective-permute-start | bytes 3145736 | tf_op jit(solution)/shard_map/ppermute | solution.py:31
  30.9 2.0 %collective-permute-start.15 = (bf16[40,16,256]{2,1,0:T(8,128)(2,1)S(1)}, bf16[40,16,256]{2,1,0:T(8,128)(2,1)S(1)}, u32[]{:S(2)}, u32[]{:S(2)}) collective-permute-start(bf16[40,16,256]{2,1,0:T(8,128)(2,1)S(1)} %pad_maximum_fusion.2.rest_8_.rest_0_), channel_id=1, source_target_pairs={{0,8},{1,9},{2,10},{3,11},{4,12},{5,13},{6,14},{7,15},{8,0},{9,1},... | collective-permute-start | bytes 983048 | tf_op jit(solution)/shard_map/ppermute | solution.py:27
  32.8 1.5 collective-permute-start.14
  34.4 14.0 %collective-permute-done.16.rest_11_.rest_3_ = bf16[40,16,256]{2,1,0:T(8,128)(2,1)S(1)} collective-permute-done((bf16[40,16,256]{2,1,0:T(8,128)(2,1)S(1)}, bf16[40,16,256]{2,1,0:T(8,128)(2,1)S(1)}, u32[]{:S(2)}, u32[]{:S(2)}) %collective-permute-start.16) | collective-permute-done | bytes 327712 | tf_op jit(solution)/shard_map/ppermute | solution.py:27
  51.9 19.3 %shard_map.73 = (bf16[4,2,16,16,256]{4,3,2,1,0:T(8,128)(2,1)}, f32[4,2,16,16,256]{4,3,2,1,0:T(8,128)}) custom-call(s32[4]{0:T(128)} %ms_ref.7, s32[128]{0:T(128)} %li_ref.7, s32[2]{0:T(128)} %pad_add_fusion.ids_ref, f32[4,5]{1,0:T(4,128)} %w_ref.7, bf16[4,2,16,256,256]{4,3,2,1,0:T(8,128)(2,1)} %q_ref.3, bf16[4,2,16,256,256]{4,3,2,1,0:T(8,128)(2,1)} %q_ref.3, ...), custom_call_target="tpu_custom_call" | custom-call | tf_op jit(solution)/shard_map/pallas_call | solution.py:130
  72.7 6.8 %shard_map.75 = (bf16[4,2,6,16,256]{4,3,2,1,0:T(8,128)(2,1)}, f32[4,2,6,16,256]{4,3,2,1,0:T(8,128)}) custom-call(s32[4]{0:T(128)} %ms_ref.7, s32[128]{0:T(128)} %li_ref.7, s32[2]{0:T(128)} %pad_add_fusion.ids_ref, f32[4,5]{1,0:T(4,128)} %w_ref.7, bf16[4,2,256,256]{3,2,1,0:T(8,128)(2,1)} %collective-permute-done.9.above_ref, ...), custom_call_target="tpu_custom_call" | custom-call | tf_op jit(solution)/shard_map/pallas_call | solution.py:235
  80.1 6.7 %shard_map.74 = (bf16[4,2,6,16,256]{4,3,2,1,0:T(8,128)(2,1)}, f32[4,2,6,16,256]{4,3,2,1,0:T(8,128)}) custom-call(s32[4]{0:T(128)} %ms_ref.7, s32[128]{0:T(128)} %li_ref.7, s32[2]{0:T(128)} %pad_add_fusion.ids_ref, f32[4,5]{1,0:T(4,128)} %w_ref.7, bf16[4,2,256,256]{3,2,1,0:T(8,128)(2,1)} %collective-permute-done.9.above_ref, ...), custom_call_target="tpu_custom_call" | custom-call | tf_op jit(solution)/shard_map/pallas_call | solution.py:235
  87.1 19.3 %shard_map.76 = (bf16[4,2,16,16,256]{4,3,2,1,0:T(8,128)(2,1)}, f32[4,2,16,16,256]{4,3,2,1,0:T(8,128)}) custom-call(s32[4]{0:T(128)} %ms_ref.7, s32[128]{0:T(128)} %li_ref.7, s32[2]{0:T(128)} %pad_add_fusion.ids_ref, f32[4,5]{1,0:T(4,128)} %w_ref.7, bf16[4,2,16,256,256]{4,3,2,1,0:T(8,128)(2,1)} %q_ref.3, bf16[4,2,16,256,256]{4,3,2,1,0:T(8,128)(2,1)} %q_ref.3, ...), custom_call_target="tpu_custom_call" | custom-call | tf_op jit(solution)/shard_map/pallas_call | solution.py:130
  108.8 1.6 %convert_add_fusion.1 = f32[4,2,16,16,256]{4,3,2,1,0:T(8,128)S(1)} fusion(f32[4,2,16,16,256]{4,3,2,1,0:T(8,128)S(1)} %copy-done.11, bf16[4,2,16,16,256]{4,3,2,1,0:T(8,128)(2,1)} %collective-permute-done.8), kind=kLoop, calls=%fused_computation.2 | loop fusion | flops 1048576 | bytes 5242880 | tf_op jit(solution)/shard_map/add | solution.py:308
  111.4 3.6 %collective-permute-start.25 = (bf16[2,20,16,256]{3,2,1,0:T(8,128)(2,1)S(1)}, bf16[2,20,16,256]{3,2,1,0:T(8,128)(2,1)S(1)}, u32[]{:S(2)}, u32[]{:S(2)}) collective-permute-start(bf16[2,20,16,256]{3,2,1,0:T(8,128)(2,1)S(1)} %get-tuple-element.26), channel_id=1, source_target_pairs={{0,8},{1,9},{2,10},{3,11},{4,12},{5,13},{6,14},{7,15},{8,0},{9,1},... | collective-permute-start | bytes 983048 | tf_op jit(solution)/shard_map/ppermute | solution.py:27
  116.8 2.1 %collective-permute-start.30 = (bf16[2,16,16,256]{3,2,1,0:T(8,128)(2,1)S(1)}, bf16[2,16,16,256]{3,2,1,0:T(8,128)(2,1)S(1)}, u32[]{:S(2)}, u32[]{:S(2)}) collective-permute-start(bf16[2,16,16,256]{3,2,1,0:T(8,128)(2,1)S(1)} %get-tuple-element.28), channel_id=1, source_target_pairs={{0,4},{1,5},{2,6},{3,7},{4,8},{5,9},{6,10},{7,11},{8,12},{9,13},{1... | collective-permute-start | bytes 786440 | tf_op jit(solution)/shard_map/ppermute | solution.py:27
  119.4 4.2 %collective-permute-done.23 = bf16[2,20,16,256]{3,2,1,0:T(8,128)(2,1)S(1)} collective-permute-done((bf16[2,20,16,256]{3,2,1,0:T(8,128)(2,1)S(1)}, bf16[2,20,16,256]{3,2,1,0:T(8,128)(2,1)S(1)}, u32[]{:S(2)}, u32[]{:S(2)}) %collective-permute-start.23) | collective-permute-done | bytes 327712 | tf_op jit(solution)/shard_map/ppermute | solution.py:27
  124.1 6.5 %collective-permute-done.25 = bf16[2,20,16,256]{3,2,1,0:T(8,128)(2,1)S(1)} collective-permute-done((bf16[2,20,16,256]{3,2,1,0:T(8,128)(2,1)S(1)}, bf16[2,20,16,256]{3,2,1,0:T(8,128)(2,1)S(1)}, u32[]{:S(2)}, u32[]{:S(2)}) %collective-permute-start.25) | collective-permute-done | bytes 327712 | tf_op jit(solution)/shard_map/ppermute | solution.py:27
  131.0 2.9 %collective-permute-start.26 = (bf16[20,16,256]{2,1,0:T(8,128)(2,1)S(1)}, bf16[20,16,256]{2,1,0:T(8,128)(2,1)S(1)}, u32[]{:S(2)}, u32[]{:S(2)}) collective-permute-start(bf16[20,16,256]{2,1,0:T(8,128)(2,1)S(1)} %fusion.10), channel_id=1, source_target_pairs={{0,2},{1,3},{2,0},{3,1},{4,6},{5,7},{6,4},{7,5},{8,10},{9,11},{10,... | collective-permute-start | bytes 491528 | tf_op jit(solution)/shard_map/ppermute | solution.py:27
  134.7 6.4 %collective-permute-done.32 = bf16[2,16,16,256]{3,2,1,0:T(8,128)(2,1)S(1)} collective-permute-done((bf16[2,16,16,256]{3,2,1,0:T(8,128)(2,1)S(1)}, bf16[2,16,16,256]{3,2,1,0:T(8,128)(2,1)S(1)}, u32[]{:S(2)}, u32[]{:S(2)}) %collective-permute-start.32) | collective-permute-done | bytes 262176 | tf_op jit(solution)/shard_map/ppermute | solution.py:27
  141.3 2.9 %collective-permute-start.33 = (bf16[16,16,256]{2,1,0:T(8,128)(2,1)S(1)}, bf16[16,16,256]{2,1,0:T(8,128)(2,1)S(1)}, u32[]{:S(2)}, u32[]{:S(2)}) collective-permute-start(bf16[16,16,256]{2,1,0:T(8,128)(2,1)S(1)} %fusion.11), channel_id=1, source_target_pairs={{0,2},{1,3},{2,0},{3,1},{4,6},{5,7},{6,4},{7,5},{8,10},{9,11},{10,... | collective-permute-start | bytes 393224 | tf_op jit(solution)/shard_map/ppermute | solution.py:27
  144.3 4.4 %collective-permute-start.27 = (f32[2,16,256]{2,1,0:T(8,128)S(1)}, f32[2,16,256]{2,1,0:T(8,128)S(1)}, u32[]{:S(2)}, u32[]{:S(2)}) collective-permute-start(f32[2,16,256]{2,1,0:T(8,128)S(1)} %get-tuple-element.41), channel_id=1, source_target_pairs={{0,16},{16,32},{32,48},{48,64},{64,80},{80,96},{96,112},{1,17},{17... | collective-permute-start | bytes 98312 | tf_op jit(solution)/shard_map/ppermute | solution.py:31
  150.3 5.9 %collective-permute-done.28 = f32[2,16,256]{2,1,0:T(8,128)S(1)} collective-permute-done((f32[2,16,256]{2,1,0:T(8,128)S(1)}, f32[2,16,256]{2,1,0:T(8,128)S(1)}, u32[]{:S(2)}, u32[]{:S(2)}) %collective-permute-start.28) | collective-permute-done | bytes 32800 | tf_op jit(solution)/shard_map/ppermute | solution.py:31
  (130 shorter events, 22.9 us)
Async XLA Ops:
  10.0 9.1 %collective-permute-start.13 = (bf16[20,16,256]{2,1,0:T(8,128)(2,1)S(1)}, bf16[20,16,256]{2,1,0:T(8,128)(2,1)S(1)}, u32[]{:S(2)}, u32[]{:S(2)}) collective-permute-start(bf16[20,16,256]{2,1,0:T(8,128)(2,1)S(1)} %pad_maximum_fusion.4), channel_id=1, source_target_pairs={{0,2},{1,3},{2,0},{3,1},{4,6},{5,7},{6,4},{7,5},{8,10},{9,11},{10,... | collective-permute-start | bytes 491528 | tf_op jit(solution)/shard_map/ppermute | solution.py:27
  13.3 9.0 %collective-permute-start.4 = (bf16[32,16,256]{2,1,0:T(8,128)(2,1)S(1)}, bf16[32,16,256]{2,1,0:T(8,128)(2,1)S(1)}, u32[]{:S(2)}, u32[]{:S(2)}) collective-permute-start(bf16[32,16,256]{2,1,0:T(8,128)(2,1)S(1)} %pad_maximum_fusion.3.rest_0_), channel_id=1, source_target_pairs={{0,1},{1,0},{2,3},{3,2},{4,5},{5,4},{6,7},{7,6},{8,9},{9,8},{10,11... | collective-permute-start | bytes 786440 | tf_op jit(solution)/shard_map/ppermute | solution.py:27
  13.4 10.3 %collective-permute-start.3 = (bf16[32,16,256]{2,1,0:T(8,128)(2,1)S(1)}, bf16[32,16,256]{2,1,0:T(8,128)(2,1)S(1)}, u32[]{:S(2)}, u32[]{:S(2)}) collective-permute-start(bf16[32,16,256]{2,1,0:T(8,128)(2,1)S(1)} %pad_maximum_fusion.3.rest_0_), channel_id=1, source_target_pairs={{0,4},{1,5},{2,6},{3,7},{4,8},{5,9},{6,10},{7,11},{8,12},{9,13},{1... | collective-permute-start | bytes 786440 | tf_op jit(solution)/shard_map/ppermute | solution.py:27
  14.9 15.3 %collective-permute-start.2 = (bf16[32,16,256]{2,1,0:T(8,128)(2,1)S(1)}, bf16[32,16,256]{2,1,0:T(8,128)(2,1)S(1)}, u32[]{:S(2)}, u32[]{:S(2)}) collective-permute-start(bf16[32,16,256]{2,1,0:T(8,128)(2,1)S(1)} %pad_maximum_fusion.3.rest_0_), channel_id=1, source_target_pairs={{0,8},{1,9},{2,10},{3,11},{4,12},{5,13},{6,14},{7,15},{8,0},{9,1},... | collective-permute-start | bytes 786440 | tf_op jit(solution)/shard_map/ppermute | solution.py:27
  17.7 13.2 %collective-permute-start.1 = (bf16[32,16,256]{2,1,0:T(8,128)(2,1)S(1)}, bf16[32,16,256]{2,1,0:T(8,128)(2,1)S(1)}, u32[]{:S(2)}, u32[]{:S(2)}) collective-permute-start(bf16[32,16,256]{2,1,0:T(8,128)(2,1)S(1)} %pad_maximum_fusion.3.rest_0_), channel_id=1, source_target_pairs={{0,12},{1,13},{2,14},{3,15},{4,0},{5,1},{6,2},{7,3},{8,4},{9,5},{1... | collective-permute-start | bytes 786440 | tf_op jit(solution)/shard_map/ppermute | solution.py:27
  19.2 13.7 %collective-permute-start.17 = (bf16[40,16,256]{2,1,0:T(8,128)(2,1)S(1)}, bf16[40,16,256]{2,1,0:T(8,128)(2,1)S(1)}, u32[]{:S(2)}, u32[]{:S(2)}) collective-permute-start(bf16[40,16,256]{2,1,0:T(8,128)(2,1)S(1)} %pad_maximum_fusion.2.rest_8_.rest_0_), channel_id=1, source_target_pairs={{0,1},{1,0},{2,3},{3,2},{4,5},{5,4},{6,7},{7,6},{8,9},{9,8},{10,11... | collective-permute-start | bytes 983048 | tf_op jit(solution)/shard_map/ppermute | solution.py:27
  22.3 49.2 %collective-permute-start.10 = (bf16[4,2,256,256]{3,2,1,0:T(8,128)(2,1)}, bf16[4,2,256,256]{3,2,1,0:T(8,128)(2,1)S(1)}, u32[]{:S(2)}, u32[]{:S(2)}) collective-permute-start(bf16[4,2,256,256]{3,2,1,0:T(8,128)(2,1)} %get-tuple-element.21), channel_id=1, source_target_pairs={{16,0},{32,16},{48,32},{64,48},{80,64},{96,80},{112,96},{17,1},{33... | collective-permute-start | bytes 3145736 | tf_op jit(solution)/shard_map/ppermute | solution.py:31
  23.7 47.9 %collective-permute-start.9 = (bf16[4,2,256,256]{3,2,1,0:T(8,128)(2,1)}, bf16[4,2,256,256]{3,2,1,0:T(8,128)(2,1)}, u32[]{:S(2)}, u32[]{:S(2)}) collective-permute-start(bf16[4,2,256,256]{3,2,1,0:T(8,128)(2,1)} %get-tuple-element.22), channel_id=1, source_target_pairs={{0,16},{16,32},{32,48},{48,64},{64,80},{80,96},{96,112},{1,17},{17... | collective-permute-start | bytes 3145736 | tf_op jit(solution)/shard_map/ppermute | solution.py:31
  30.3 18.0 %collective-permute-start.16 = (bf16[40,16,256]{2,1,0:T(8,128)(2,1)S(1)}, bf16[40,16,256]{2,1,0:T(8,128)(2,1)S(1)}, u32[]{:S(2)}, u32[]{:S(2)}) collective-permute-start(bf16[40,16,256]{2,1,0:T(8,128)(2,1)S(1)} %pad_maximum_fusion.2.rest_8_.rest_0_), channel_id=1, source_target_pairs={{0,4},{1,5},{2,6},{3,7},{4,8},{5,9},{6,10},{7,11},{8,12},{9,13},{1... | collective-permute-start | bytes 983048 | tf_op jit(solution)/shard_map/ppermute | solution.py:27
  30.9 17.4 %collective-permute-start.15 = (bf16[40,16,256]{2,1,0:T(8,128)(2,1)S(1)}, bf16[40,16,256]{2,1,0:T(8,128)(2,1)S(1)}, u32[]{:S(2)}, u32[]{:S(2)}) collective-permute-start(bf16[40,16,256]{2,1,0:T(8,128)(2,1)S(1)} %pad_maximum_fusion.2.rest_8_.rest_0_), channel_id=1, source_target_pairs={{0,8},{1,9},{2,10},{3,11},{4,12},{5,13},{6,14},{7,15},{8,0},{9,1},... | collective-permute-start | bytes 983048 | tf_op jit(solution)/shard_map/ppermute | solution.py:27
  32.8 16.1 %collective-permute-start.14 = (bf16[40,16,256]{2,1,0:T(8,128)(2,1)S(1)}, bf16[40,16,256]{2,1,0:T(8,128)(2,1)S(1)}, u32[]{:S(2)}, u32[]{:S(2)}) collective-permute-start(bf16[40,16,256]{2,1,0:T(8,128)(2,1)S(1)} %pad_maximum_fusion.2.rest_8_.rest_0_), channel_id=1, source_target_pairs={{0,12},{1,13},{2,14},{3,15},{4,0},{5,1},{6,2},{7,3},{8,4},{9,5},{1... | collective-permute-start | bytes 983048 | tf_op jit(solution)/shard_map/ppermute | solution.py:27
  49.9 21.4 %collective-permute-start.20 = (bf16[40,16,256]{2,1,0:T(8,128)(2,1)S(1)}, bf16[40,16,256]{2,1,0:T(8,128)(2,1)S(1)}, u32[]{:S(2)}, u32[]{:S(2)}) collective-permute-start(bf16[40,16,256]{2,1,0:T(8,128)(2,1)S(1)} %collective-permute-done.16.rest_11_.rest_3_), channel_id=1, source_target_pairs={{0,1},{1,0},{2,3},{3,2},{4,5},{5,4},{6,7},{7,6},{8,9},{9,8},{10,11... | collective-permute-start | bytes 983048 | tf_op jit(solution)/shard_map/ppermute | solution.py:27
  50.2 21.3 %collective-permute-start.19 = (bf16[40,16,256]{2,1,0:T(8,128)(2,1)S(1)}, bf16[40,16,256]{2,1,0:T(8,128)(2,1)S(1)}, u32[]{:S(2)}, u32[]{:S(2)}) collective-permute-start(bf16[40,16,256]{2,1,0:T(8,128)(2,1)S(1)} %collective-permute-done.15.rest_10_.rest_2_), channel_id=1, source_target_pairs={{0,1},{1,0},{2,3},{3,2},{4,5},{5,4},{6,7},{7,6},{8,9},{9,8},{10,11... | collective-permute-start | bytes 983048 | tf_op jit(solution)/shard_map/ppermute | solution.py:27
  50.6 20.9 %collective-permute-start.18 = (bf16[40,16,256]{2,1,0:T(8,128)(2,1)S(1)}, bf16[40,16,256]{2,1,0:T(8,128)(2,1)S(1)}, u32[]{:S(2)}, u32[]{:S(2)}) collective-permute-start(bf16[40,16,256]{2,1,0:T(8,128)(2,1)S(1)} %collective-permute-done.14.rest_9_.rest_1_), channel_id=1, source_target_pairs={{0,1},{1,0},{2,3},{3,2},{4,5},{5,4},{6,7},{7,6},{8,9},{9,8},{10,11... | collective-permute-start | bytes 983048 | tf_op jit(solution)/shard_map/ppermute | solution.py:27
  71.3 36.4 %collective-permute-start.8 = (bf16[4,2,16,16,256]{4,3,2,1,0:T(8,128)(2,1)}, bf16[4,2,16,16,256]{4,3,2,1,0:T(8,128)(2,1)}, u32[]{:S(2)}, u32[]{:S(2)}) collective-permute-start(bf16[4,2,16,16,256]{4,3,2,1,0:T(8,128)(2,1)} %get-tuple-element.14), channel_id=1, source_target_pairs={{0,1},{1,0},{2,3},{3,2},{4,5},{5,4},{6,7},{7,6},{8,9},{9,8},{10,11... | collective-permute-start | bytes 3145736 | tf_op jit(solution)/shard_map/ppermute | solution.py:27
  79.5 27.4 %collective-permute-start.22 = (bf16[4,2,6,16,256]{4,3,2,1,0:T(8,128)(2,1)}, bf16[4,2,6,16,256]{4,3,2,1,0:T(8,128)(2,1)S(1)}, u32[]{:S(2)}, u32[]{:S(2)}) collective-permute-start(bf16[4,2,6,16,256]{4,3,2,1,0:T(8,128)(2,1)} %get-tuple-element.18), channel_id=1, source_target_pairs={{0,1},{1,0},{2,3},{3,2},{4,5},{5,4},{6,7},{7,6},{8,9},{9,8},{10,11... | collective-permute-start | bytes 1179656 | tf_op jit(solution)/shard_map/ppermute | solution.py:27
  86.9 20.1 %collective-permute-start.21 = (bf16[4,2,6,16,256]{4,3,2,1,0:T(8,128)(2,1)}, bf16[4,2,6,16,256]{4,3,2,1,0:T(8,128)(2,1)S(1)}, u32[]{:S(2)}, u32[]{:S(2)}) collective-permute-start(bf16[4,2,6,16,256]{4,3,2,1,0:T(8,128)(2,1)} %get-tuple-element.16), channel_id=1, source_target_pairs={{0,1},{1,0},{2,3},{3,2},{4,5},{5,4},{6,7},{7,6},{8,9},{9,8},{10,11... | collective-permute-start | bytes 1179656 | tf_op jit(solution)/shard_map/ppermute | solution.py:27
  111.1 12.6 %collective-permute-start.23 = (bf16[2,20,16,256]{3,2,1,0:T(8,128)(2,1)S(1)}, bf16[2,20,16,256]{3,2,1,0:T(8,128)(2,1)S(1)}, u32[]{:S(2)}, u32[]{:S(2)}) collective-permute-start(bf16[2,20,16,256]{3,2,1,0:T(8,128)(2,1)S(1)} %get-tuple-element.25), channel_id=1, source_target_pairs={{0,4},{1,5},{2,6},{3,7},{4,8},{5,9},{6,10},{7,11},{8,12},{9,13},{1... | collective-permute-start | bytes 983048 | tf_op jit(solution)/shard_map/ppermute | solution.py:27
  111.4 19.2 %collective-permute-start.25 = (bf16[2,20,16,256]{3,2,1,0:T(8,128)(2,1)S(1)}, bf16[2,20,16,256]{3,2,1,0:T(8,128)(2,1)S(1)}, u32[]{:S(2)}, u32[]{:S(2)}) collective-permute-start(bf16[2,20,16,256]{3,2,1,0:T(8,128)(2,1)S(1)} %get-tuple-element.26), channel_id=1, source_target_pairs={{0,8},{1,9},{2,10},{3,11},{4,12},{5,13},{6,14},{7,15},{8,0},{9,1},... | collective-permute-start | bytes 983048 | tf_op jit(solution)/shard_map/ppermute | solution.py:27
  115.0 15.8 %collective-permute-start.24 = (bf16[2,20,16,256]{3,2,1,0:T(8,128)(2,1)S(1)}, bf16[2,20,16,256]{3,2,1,0:T(8,128)(2,1)S(1)}, u32[]{:S(2)}, u32[]{:S(2)}) collective-permute-start(bf16[2,20,16,256]{3,2,1,0:T(8,128)(2,1)S(1)} %get-tuple-element.27), channel_id=1, source_target_pairs={{0,12},{1,13},{2,14},{3,15},{4,0},{5,1},{6,2},{7,3},{8,4},{9,5},{1... | collective-permute-start | bytes 983048 | tf_op jit(solution)/shard_map/ppermute | solution.py:27
  116.8 17.9 %collective-permute-start.30 = (bf16[2,16,16,256]{3,2,1,0:T(8,128)(2,1)S(1)}, bf16[2,16,16,256]{3,2,1,0:T(8,128)(2,1)S(1)}, u32[]{:S(2)}, u32[]{:S(2)}) collective-permute-start(bf16[2,16,16,256]{3,2,1,0:T(8,128)(2,1)S(1)} %get-tuple-element.28), channel_id=1, source_target_pairs={{0,4},{1,5},{2,6},{3,7},{4,8},{5,9},{6,10},{7,11},{8,12},{9,13},{1... | collective-permute-start | bytes 786440 | tf_op jit(solution)/shard_map/ppermute | solution.py:27
  118.9 22.3 %collective-permute-start.32 = (bf16[2,16,16,256]{3,2,1,0:T(8,128)(2,1)S(1)}, bf16[2,16,16,256]{3,2,1,0:T(8,128)(2,1)S(1)}, u32[]{:S(2)}, u32[]{:S(2)}) collective-permute-start(bf16[2,16,16,256]{3,2,1,0:T(8,128)(2,1)S(1)} %get-tuple-element.29), channel_id=1, source_target_pairs={{0,8},{1,9},{2,10},{3,11},{4,12},{5,13},{6,14},{7,15},{8,0},{9,1},... | collective-permute-start | bytes 786440 | tf_op jit(solution)/shard_map/ppermute | solution.py:27
  123.6 17.5 %collective-permute-start.31 = (bf16[2,16,16,256]{3,2,1,0:T(8,128)(2,1)S(1)}, bf16[2,16,16,256]{3,2,1,0:T(8,128)(2,1)S(1)}, u32[]{:S(2)}, u32[]{:S(2)}) collective-permute-start(bf16[2,16,16,256]{3,2,1,0:T(8,128)(2,1)S(1)} %get-tuple-element.30), channel_id=1, source_target_pairs={{0,12},{1,13},{2,14},{3,15},{4,0},{5,1},{6,2},{7,3},{8,4},{9,5},{1... | collective-permute-start | bytes 786440 | tf_op jit(solution)/shard_map/ppermute | solution.py:27
  131.0 13.2 %collective-permute-start.26 = (bf16[20,16,256]{2,1,0:T(8,128)(2,1)S(1)}, bf16[20,16,256]{2,1,0:T(8,128)(2,1)S(1)}, u32[]{:S(2)}, u32[]{:S(2)}) collective-permute-start(bf16[20,16,256]{2,1,0:T(8,128)(2,1)S(1)} %fusion.10), channel_id=1, source_target_pairs={{0,2},{1,3},{2,0},{3,1},{4,6},{5,7},{6,4},{7,5},{8,10},{9,11},{10,... | collective-permute-start | bytes 491528 | tf_op jit(solution)/shard_map/ppermute | solution.py:27
  (33 other events, 297.6 us)
